TPU v7x, 128 devices: a whole 4x4x4 slice. The times are simulated.
128 devices in a mesh: epoch: 8 (over z_lo, x), strip: 16 (over z_hi, y, core).
Axes of the slice: x: 4, y: 4, z: 4 (z_hi: 2, z_lo: 2; z = z_hi * 2 + z_lo), core: 2. Of those that a mesh axis runs over, the one named last changes fastest.
Arguments:
- raw_tiles: float32 [8, 192, 256, 512], P('epoch', 'strip'), may hold values from -6 to 6
- tile_kind: int32 [8, 192], P('epoch', 'strip'), may hold values from 0 to 3
- tile_invvar: float32 [8, 192], P('epoch', 'strip'), may hold values from 0.2 to 5
- tile_heights: int32 [8, 8, 24], P('epoch'), may hold values from 1 to 256, 4096 in all within a row
- row_interp: float32 [4, 256, 256], replicated, may hold values from -0.4 to 1.9
- col_interp: float32 [4, 512, 512], replicated, may hold values from -0.4 to 1.9
- psf_profiles: float32 [2, 2, 31], replicated, may hold values from -1 to 1
- psf_poly: float32 [8, 2, 6], replicated, may hold values from -1 to 1
Outputs:
- difference: float32 [8, 4096, 4096], P('epoch', 'strip')
Inputs may be any that keep to these rules, and one draw needn't show every extreme that they name: `tile_heights`: along the last dimension, the heights of one column block's tiles from the top of the patch down; they sum to 4096, and the tallest is exactly 256.
All inputs are finite; a program needn't handle non-finite values.
Results may differ from a plain program's by a relative error of at most 0.0003.
Values sent between devices are 32-bit elements; how exact they have to be, the bound alone decides.
A program may use at most 128 MiB of HBM per device.

v0:
```python
import math

import jax
import jax.numpy as jnp
from jax import lax
from jax.sharding import PartitionSpec as P

ROWS_DEV = 256
KSIZE = 31


precise = lax.Precision.HIGHEST


def swapped(value, axis, apart):
    mask = 2**apart
    pairs = [(source, source ^ mask) for source in range(lax.axis_size(axis))]
    return lax.ppermute(value, axis, pairs)


def side_by_side(arrays, axis, split_dim, concat_dim, along):
    widths = [math.prod(a.shape[along:]) for a in arrays]
    both = jnp.concatenate(
        [a.reshape(*a.shape[:along], w) for a, w in zip(arrays, widths)], axis=along
    )
    whole = lax.all_to_all(both, axis, split_axis=split_dim, concat_axis=concat_dim, tiled=True)
    tiles = jnp.split(whole, [sum(widths[:k]) for k in range(1, len(widths))], axis=along)
    return tuple((b.reshape(*whole.shape[:along], *a.shape[along:]) for a, b in zip(arrays, tiles)))


def cut_along(value, dim, count):
    before, after = (value.shape[:dim], value.shape[dim + 1 :])
    return jnp.moveaxis(value.reshape(*before, count, -1, *after), dim, 0)


def sum_at_owner(value, axis, dim):
    count = lax.axis_size(axis)
    tiles = lax.all_to_all(cut_along(value, dim, count), axis, 0, 0, tiled=True)
    return jnp.sum(tiles, axis=0)


def padded_2(value, sides, width):
    for axis, dim in sides:
        count, length = (lax.axis_size(axis), value.shape[dim])
        up = [(i, (i + 1) % count) for i in range(count - 1)]
        down = [(j, i) for i, j in up]
        last = lax.slice_in_dim(value, length - width, length, axis=dim)
        initial = lax.slice_in_dim(value, 0, width, axis=dim)
        before = lax.ppermute(last, axis, up)
        after = lax.ppermute(initial, axis, down)
        value = jnp.concatenate([before, value, after], axis=dim)
    return value


def positions(first_cell, length, extent):
    counter = (first_cell + jnp.arange(length)).astype(jnp.float32)
    return (2.0 * counter + 1.0) / extent - 1.0


def coeff_maps(poly_rows, row_coords, col_coords):
    row_term = row_coords[:, None]
    col_term = col_coords[None, :]
    terms = poly_rows[..., None, None]
    return (
        terms[..., 0, :, :]
        + terms[..., 1, :, :] * row_term
        + terms[..., 2, :, :] * col_term
        + terms[..., 3, :, :] * row_term * row_term
        + terms[..., 4, :, :] * row_term * col_term
        + terms[..., 5, :, :] * col_term * col_term
    )


def row_pass(padded, profiles):
    margin = KSIZE // 2
    rows_out = padded.shape[0] - 2 * margin
    offset = jnp.arange(padded.shape[0])[None, :] - jnp.arange(rows_out)[:, None]
    onehot = (offset[:, :, None] == jnp.arange(KSIZE)[None, None, :]).astype(jnp.float32)
    banded = jnp.einsum("rqi,ki->krq", onehot, profiles[:, 0, :], precision=precise)
    return jnp.einsum("krq,qc->krc", banded, padded, precision=precise)


def col_pass(padded, profiles):
    margin = KSIZE // 2
    basis_count, rows_out, wide_in = padded.shape
    width_out = wide_in - 2 * margin
    block_cols = 128
    block_count = width_out // block_cols
    extended = jnp.pad(padded, ((0, 0), (0, 0), (0, block_cols - 2 * margin)))
    leading = extended[:, :, :width_out].reshape(basis_count, rows_out, block_count, block_cols)
    trailing = extended[:, :, block_cols : block_cols + width_out].reshape(
        basis_count, rows_out, block_count, block_cols
    )
    window = jnp.concatenate([leading, trailing[:, :, :, : 2 * margin]], axis=3)
    offset = jnp.arange(block_cols + 2 * margin)[:, None] - jnp.arange(block_cols)[None, :]
    onehot = (offset[:, :, None] == jnp.arange(KSIZE)[None, None, :]).astype(jnp.float32)
    toeplitz = jnp.einsum("mci,ki->kmc", onehot, profiles[:, 1, :], precision=precise)
    result = jnp.einsum("krnm,kmc->krnc", window, toeplitz, precision=precise)
    return result.reshape(basis_count, rows_out, width_out)


def shards(
    raw_tiles, tile_kind, tile_invvar, tile_heights, row_interp, col_interp, psf_profiles, psf_poly
):
    strips = lax.axis_size("strip")
    strip_index = lax.axis_index("strip")
    tiles_dev = raw_tiles.shape[1]
    tile_rows = raw_tiles.shape[2]
    tile_cols = raw_tiles.shape[3]
    blocks = tile_heights.shape[1]
    per_col = tile_heights.shape[2]
    ncol_all = blocks * tile_cols
    nrow_all = ROWS_DEV * strips
    sources = strips // blocks
    first_tile = strip_index * tiles_dev
    block_index = first_tile // per_col
    column_heights = lax.dynamic_index_in_dim(tile_heights[0], block_index, 0, keepdims=False)
    column_starts = jnp.cumsum(column_heights) - column_heights
    offset_in = first_tile % per_col
    my_heights = lax.dynamic_slice_in_dim(column_heights, offset_in, tiles_dev)
    my_starts = lax.dynamic_slice_in_dim(column_starts, offset_in, tiles_dev)
    live_rows = jnp.arange(tile_rows)[None, :] < my_heights[:, None]
    masked = jnp.where(live_rows[:, :, None], raw_tiles[0], 0.0)
    tile_kinds = tile_kind[0]
    half_warped = jnp.einsum(
        "tij,tjk->tik", jnp.take(row_interp, tile_kinds, axis=0), masked, precision=precise
    )
    warped = jnp.einsum(
        "tik,tlk->til", half_warped, jnp.take(col_interp, tile_kinds, axis=0), precision=precise
    )
    sky_rows = jnp.arange(nrow_all)
    covering = jnp.sum((sky_rows[:, None] >= my_starts[None, :]).astype(jnp.int32), axis=1) - 1
    chosen = jnp.maximum(covering, 0)
    member = chosen[:, None] == jnp.arange(tiles_dev)[None, :]
    start_of = jnp.sum(jnp.where(member, my_starts[None, :], 0), axis=1)
    height_of = jnp.sum(jnp.where(member, my_heights[None, :], 0), axis=1)
    weight_of = jnp.sum(jnp.where(member, tile_invvar[0][None, :], 0.0), axis=1)
    local_row = sky_rows - start_of
    covered = (covering >= 0) & (local_row < height_of)
    source = chosen * tile_rows + jnp.clip(local_row, 0, tile_rows - 1)
    picked = jnp.take(warped.reshape(tiles_dev * tile_rows, tile_cols), source, axis=0)
    outgoing = jnp.where(covered[:, None], picked, 0.0).reshape(strips, ROWS_DEV, tile_cols)
    out_weight = jnp.where(covered, weight_of, 0.0).reshape(strips, ROWS_DEV)
    half_cols = tile_cols // 2
    pair_side = strip_index % 2
    kept = lax.dynamic_slice_in_dim(outgoing, pair_side * half_cols, half_cols, 2)
    given = lax.dynamic_slice_in_dim(outgoing, (1 - pair_side) * half_cols, half_cols, 2)
    partner_part, partner_weight = swapped((given, out_weight), "strip", 0)
    kept = kept + partner_part
    pair_weight = out_weight + partner_weight
    incoming, in_weight = side_by_side((kept, pair_weight), "strip", 0, 0, 2)
    piece_cols = kept.shape[2]
    arranged = jnp.transpose(incoming.reshape(blocks, sources, ROWS_DEV, piece_cols), (2, 0, 1, 3))
    science_blocks = arranged.reshape(ROWS_DEV, blocks, tile_cols)
    weights = jnp.transpose(in_weight.reshape(blocks, sources, ROWS_DEV)[:, 0, :])
    weighted = (science_blocks * weights[:, :, None]).reshape(ROWS_DEV, ncol_all)
    science = science_blocks.reshape(ROWS_DEV, ncol_all)
    row_coords = positions(strip_index * ROWS_DEV, ROWS_DEV, nrow_all)
    epochs = lax.axis_size("epoch")
    share_cols = ncol_all // epochs
    weighted_sum, weight_sum = (
        sum_at_owner(weighted, "epoch", 1),
        sum_at_owner(weights, "epoch", 1),
    )
    template = (
        weighted_sum.reshape(ROWS_DEV, blocks // epochs, tile_cols) / weight_sum[:, :, None]
    ).reshape(ROWS_DEV, share_cols)
    padded = padded_2(template, (("epoch", 1), ("strip", 0)), KSIZE // 2)
    convolved = col_pass(row_pass(padded, psf_profiles), psf_profiles)
    col_coords = positions(lax.axis_index("epoch") * share_cols, share_cols, ncol_all)
    coeffs = coeff_maps(psf_poly, row_coords, col_coords)
    matched = coeffs[:, 0] * convolved[0][None] + coeffs[:, 1] * convolved[1][None]
    returned = lax.all_to_all(matched, "epoch", split_axis=0, concat_axis=2, tiled=True)
    return science[None] - returned


def solution(mesh):
    in_specs = (
        P("epoch", "strip", None, None),
        P("epoch", "strip"),
        P("epoch", "strip"),
        P("epoch", None, None),
        P(),
        P(),
        P(),
        P(),
    )
    out_specs = P("epoch", "strip", None)
    return jax.shard_map(shards, mesh=mesh, in_specs=in_specs, out_specs=out_specs, check_vma=False)
```

profile of v0, /device:TPU:81, one launch (start us, length us, event | category | flops | bytes accessed | tf_op | source)
XLA Modules:
  0.0 337.6 jit_solution(12560675596713833216)
XLA Ops:
  6.6 9.0 %gather_fusion.1 = f32[12,512,512]{2,1,0:T(8,128)} fusion(f32[4,512,512]{2,1,0:T(8,128)} %param.13, s32[1024]{0:T(1024)S(1)} %pad_clamp_fusion), kind=kCustom, calls=%fused_computation.1 | custom fusion | bytes 25165872 | tf_op jit(solution)/shard_map/jit(_take)/gather | solution.py:129
  15.8 8.8 %fusion.3 = f32[12,256,512]{2,1,0:T(8,128)S(1)} fusion(f32[1,12,256,512]{3,2,1,0:T(8,128)} %param.8, f32[12,256,256]{2,1,0:T(8,128)} %gather_fusion, pred[12,256]{1,0:T(8,128)(4,1)S(1)} %iota_compare_fusion.10, pred[12]{0:T(512)(128)(4,1)S(1)} %compare_and_fusion.2), kind=kOutput, calls=%fused_computation.10 | convolution fusion | flops 4834197504 | bytes 15731724 | tf_op jit(solution)/shard_map/tij,tjk->tik/dot_general | solution.py:125
  24.6 15.8 %fusion = f32[12,256,512]{2,1,0:T(8,128)} fusion(f32[12,256,512]{2,1,0:T(8,128)S(1)} %fusion.3, f32[12,512,512]{2,1,0:T(8,128)} %gather_fusion.1, pred[12]{0:T(512)(128)(4,1)S(1)} %compare_and_fusion.2), kind=kOutput, calls=%fused_computation.4 | convolution fusion | flops 9666822144 | bytes 25165836 | tf_op jit(solution)/shard_map/tik,tlk->til/dot_general | solution.py:128
  40.4 20.8 %gather_fusion.2 = f32[4096,512]{1,0:T(8,128)} fusion(f32[3072,512]{1,0:T(8,128)} %bitcast.97, s32[4096]{0:T(1024)S(1)} %broadcast_clamp_fusion), kind=kCustom, calls=%fused_computation.2 | custom fusion | bytes 16793600 | tf_op jit(solution)/shard_map/jit(_take)/gather | solution.py:141
  61.2 9.3 %copy.42 = f32[16,256,512]{1,2,0:T(8,128)} copy(f32[16,256,512]{2,1,0:T(8,128)} %bitcast.100) | data formatting | bytes 16777216 | tf_op jit(solution)/shard_map/jit(_take)/gather | solution.py:141
  70.7 4.5 %select_select_fusion = f32[16,256,512]{1,2,0:T(8,128)S(1)} fusion(f32[16,256,512]{1,2,0:T(8,128)} %copy.42, pred[16,256]{1,0:T(8,128)(4,1)S(1)} %compare_and_fusion, pred[16,256]{1,0:T(8,128)(4,1)S(1)} %get-tuple-element.8), kind=kLoop, calls=%fused_computation.8 | loop fusion | flops 4194304 | bytes 16785408 | tf_op jit(solution)/shard_map/jit(_where)/select_n | solution.py:142
  81.6 7.1 %collective-permute-done.1 = f32[16,256]{1,0:T(8,128)S(1)} collective-permute-done((f32[16,256]{1,0:T(8,128)S(1)}, f32[16,256]{1,0:T(8,128)S(1)}, u32[]{:S(2)}, u32[]{:S(2)}) %collective-permute-start.1) | collective-permute-done | bytes 16416 | tf_op jit(solution)/shard_map/ppermute | solution.py:18
  88.7 4.1 %dynamic-slice_add_fusion = f32[16,256,256]{1,2,0:T(8,128)S(1)} fusion(f32[16,256,256]{1,2,0:T(8,128)} %collective-permute-done, f32[16,256,512]{1,2,0:T(8,128)} %copy-done.2, s32[]{:T(128)S(6)} %select_n.124), kind=kLoop, calls=%fused_computation.22 | loop fusion | flops 1048576 | bytes 12582916 | tf_op jit(solution)/shard_map/add | solution.py:149
  93.2 55.4 %all_to_all.33 = f32[16,256,257]{1,2,0:T(8,128)S(1)} all-to-all(f32[16,256,257]{1,2,0:T(8,128)S(1)} %pad_maximum_fusion), channel_id=1, replica_groups=mesh['epoch'=8,'strip'=16] {'strip'}, dimensions={0} | all-to-all | bytes 8421376 | tf_op jit(solution)/shard_map/all_to_all | solution.py:26
  153.0 5.4 %copy.53 = f32[256,8,512]{2,0,1:T(8,128)} copy(f32[256,8,512]{0,2,1:T(8,128)} %bitcast.98) | data formatting | bytes 8388608 | tf_op jit(solution)/shard_map/reshape | solution.py:154
  160.0 5.0 %all-to-all-start.2 = ((f32[8,256,1]{1,2,0:T(1,128)}), f32[8,256,1]{1,2,0:T(1,128)S(1)}, u32[]{:S(2)}, u32[]{:S(2)}) async-start(f32[8,256,1]{1,2,0:T(1,128)} %copy.45), calls=%async_computation.2 | async-start | bytes 16384 | tf_op jit(solution)/shard_map/all_to_all | solution.py:38
  165.0 4.5 %multiply_bitcast_fusion = f32[8,256,512]{2,1,0:T(8,128)} fusion(f32[256,8,512]{2,0,1:T(8,128)} %copy.53, f32[256,8]{0,1:T(8,128)S(1)} %bitcast.109), kind=kLoop, calls=%fused_computation.21 | loop fusion | flops 1048576 | bytes 8396800 | tf_op jit(solution)/shard_map/transpose | solution.py:33
  170.1 4.7 %all-to-all-start.1 = ((f32[8,256,512]{2,1,0:T(8,128)}), f32[8,256,512]{2,1,0:T(8,128)}, u32[]{:S(2)}, u32[]{:S(2)}) async-start(f32[8,256,512]{2,1,0:T(8,128)} %multiply_bitcast_fusion), calls=%async_computation.1 | async-start | bytes 8388608 | tf_op jit(solution)/shard_map/all_to_all | solution.py:38
  175.0 4.8 %fusion.20 = f32[2,256,286]{2,0,1:T(2,128)S(1)} fusion(f32[2,31,1]{1,0,2:T(2,128)S(1)} %bitcast.113, s32[256,286]{1,0:T(8,128)S(1)} %iota_subtract_fusion), kind=kOutput, calls=%fused_computation.35 | convolution fusion | flops 56742400 | bytes 878840 | tf_op jit(solution)/shard_map/rqi,ki->krq/dot_general | solution.py:79
  179.9 4.3 %add_add_fusion = f32[8,2,256,512]{3,2,0,1:T(8,128)} fusion(f32[8,2,512]{2,0,1:T(8,128)S(1)} %get-tuple-element.30, f32[512]{0:T(512)S(1)} %multiply_add_fusion.1, f32[8,2,256]{2,0,1:T(8,128)S(1)} %get-tuple-element.32, f32[8,2,256]{2,0,1:T(8,128)S(1)} %get-tuple-element.33, f32[8,2,512]{2,0,1:T(8,128)S(1)} %get-tuple-element.29, ...), kind=kLoop, calls=%fused_computation.7 | loop fusion | flops 10485760 | bytes 8505344 | tf_op jit(solution)/shard_map/add | solution.py:65
  184.2 40.3 %all-to-all-done.1 = f32[8,256,512]{2,1,0:T(8,128)} async-done(((f32[8,256,512]{2,1,0:T(8,128)}), f32[8,256,512]{2,1,0:T(8,128)}, u32[]{:S(2)}, u32[]{:S(2)}) %all-to-all-start.1) | async-done | bytes 4194336 | tf_op jit(solution)/shard_map/all_to_all | solution.py:38
  227.4 10.4 %collective-permute-start.2 = (f32[256,15]{1,0:T(8,128)S(1)}, f32[256,15]{1,0:T(8,128)S(1)}, u32[]{:S(2)}, u32[]{:S(2)}) collective-permute-start(f32[256,15]{1,0:T(8,128)S(1)} %get-tuple-element.15), channel_id=1, source_target_pairs={{0,16},{16,32},{32,48},{48,64},{64,80},{80,96},{96,112},{1,17},{17... | collective-permute-start | bytes 46088 | tf_op jit(solution)/shard_map/ppermute | solution.py:49
  239.7 3.8 %collective-permute-done.3 = f32[256,15]{1,0:T(8,128)S(1)} collective-permute-done((f32[256,15]{1,0:T(8,128)S(1)}, f32[256,15]{1,0:T(8,128)S(1)}, u32[]{:S(2)}, u32[]{:S(2)}) %collective-permute-start.3) | collective-permute-done | bytes 15392 | tf_op jit(solution)/shard_map/ppermute | solution.py:50
  243.6 6.7 %collective-permute-start.4 = (f32[15,542]{1,0:T(8,128)S(1)}, f32[15,542]{1,0:T(8,128)S(1)}, u32[]{:S(2)}, u32[]{:S(2)}) collective-permute-start(f32[15,542]{1,0:T(8,128)S(1)} %get-tuple-element.13), channel_id=1, source_target_pairs={{0,1},{1,2},{2,3},{3,4},{4,5},{5,6},{6,7},{7,8},{8,9},{9,10},{10,1... | collective-permute-start | bytes 97568 | tf_op jit(solution)/shard_map/ppermute | solution.py:49
  260.0 4.6 %fusion.8 = f32[8,256,512]{2,1,0:T(8,128)S(1)} fusion(f32[8,2,256,512]{3,2,0,1:T(8,128)} %add_add_fusion, f32[256,512]{1,0:T(8,128)S(1)} %copy.49, f32[256,512]{1,0:T(8,128)S(1)} %copy.48), kind=kLoop, calls=%fused_computation.17 | loop fusion | flops 3145728 | bytes 13631488 | tf_op jit(solution)/shard_map/add | solution.py:172
  264.6 56.0 %all_to_all.34 = f32[8,256,512]{2,1,0:T(8,128)} all-to-all(f32[8,256,512]{2,1,0:T(8,128)S(1)} %fusion.8), channel_id=1, replica_groups=mesh['epoch'=8,'strip'=16] {'epoch'}, dimensions={0} | all-to-all | bytes 8388608 | tf_op jit(solution)/shard_map/all_to_all | solution.py:173
  320.6 5.3 %copy.50 = f32[8,256,512]{1,2,0:T(8,128)} copy(f32[8,256,512]{2,1,0:T(8,128)} %all_to_all.34) | data formatting | bytes 8388608 | tf_op jit(solution)/shard_map/all_to_all | solution.py:173
  326.0 6.0 %bitcast_subtract_fusion = f32[1,256,4096]{1,2,0:T(8,128)} fusion(f32[1,256,4096]{1,2,0:T(8,128)} %bitcast.101, f32[1,256,4096]{1,2,0:T(8,128)} %bitcast.99), kind=kLoop, calls=%fused_computation.20 | loop fusion | flops 1048576 | bytes 12582912 | tf_op jit(solution)/shard_map/sub | solution.py:174
  332.0 5.6 %copy.51 = f32[1,256,4096]{2,1,0:T(8,128)} copy(f32[1,256,4096]{1,2,0:T(8,128)} %bitcast_subtract_fusion) | data formatting | bytes 8388608 | tf_op jit(solution)/shard_map/sub | solution.py:174
  (80 shorter events, 35.0 us)
Async XLA Ops:
  0.0 4.2 %copy-start = (f32[4,256,256]{2,1,0:T(8,128)S(1)}, f32[4,256,256]{2,1,0:T(8,128)}, u32[]{:S(2)}) copy-start(f32[4,256,256]{2,1,0:T(8,128)} %param.12) | copy-start | bytes 3145732
  61.2 9.3 %copy-start.6 = (f32[1,12]{1,0:T(1,128)S(1)}, f32[1,12]{1,0:T(1,128)}, u32[]{:S(2)}) copy-start(f32[1,12]{1,0:T(1,128)} %param.10) | copy-start | bytes 148
  75.3 3.2 copy-start.2
  80.8 7.9 %collective-permute-start = (f32[16,256,256]{1,2,0:T(8,128)}, f32[16,256,256]{1,2,0:T(8,128)}, u32[]{:S(2)}, u32[]{:S(2)}) collective-permute-start(f32[16,256,256]{1,2,0:T(8,128)} %constant_dynamic-slice_fusion), channel_id=1, source_target_pairs={{0,1},{1,0},{2,3},{3,2},{4,5},{5,4},{6,7},{7,6},{8,9},{9,8},{10,11... | collective-permute-start | bytes 12582920 | tf_op jit(solution)/shard_map/ppermute | solution.py:18
  81.6 7.1 %collective-permute-start.1 = (f32[16,256]{1,0:T(8,128)S(1)}, f32[16,256]{1,0:T(8,128)S(1)}, u32[]{:S(2)}, u32[]{:S(2)}) collective-permute-start(f32[16,256]{1,0:T(8,128)S(1)} %get-tuple-element.7), channel_id=1, source_target_pairs={{0,1},{1,0},{2,3},{3,2},{4,5},{5,4},{6,7},{7,6},{8,9},{9,8},{10,11... | collective-permute-start | bytes 49160 | tf_op jit(solution)/shard_map/ppermute | solution.py:18
  148.6 2.0 copy-start.3
  160.0 10.1 %all-to-all-start.2 = ((f32[8,256,1]{1,2,0:T(1,128)}), f32[8,256,1]{1,2,0:T(1,128)S(1)}, u32[]{:S(2)}, u32[]{:S(2)}) async-start(f32[8,256,1]{1,2,0:T(1,128)} %copy.45), calls=%async_computation.2 | async-start | bytes 16384 | tf_op jit(solution)/shard_map/all_to_all | solution.py:38
  169.5 5.4 %copy-start.5 = (f32[2,2,31]{2,1,0:T(2,128)S(1)}, f32[2,2,31]{2,1,0:T(2,128)}, u32[]{:S(2)}) copy-start(f32[2,2,31]{2,1,0:T(2,128)} %param.14) | copy-start | bytes 1492
  169.5 5.4 %copy-start.4 = (f32[8,2,6]{0,1,2:T(2,128)S(1)}, f32[8,2,6]{0,1,2:T(2,128)}, u32[]{:S(2)}) copy-start(f32[8,2,6]{0,1,2:T(2,128)} %param.15) | copy-start | bytes 1156
  170.1 54.4 %all-to-all-start.1 = ((f32[8,256,512]{2,1,0:T(8,128)}), f32[8,256,512]{2,1,0:T(8,128)}, u32[]{:S(2)}, u32[]{:S(2)}) async-start(f32[8,256,512]{2,1,0:T(8,128)} %multiply_bitcast_fusion), calls=%async_computation.1 | async-start | bytes 8388608 | tf_op jit(solution)/shard_map/all_to_all | solution.py:38
  227.4 12.3 %collective-permute-start.2 = (f32[256,15]{1,0:T(8,128)S(1)}, f32[256,15]{1,0:T(8,128)S(1)}, u32[]{:S(2)}, u32[]{:S(2)}) collective-permute-start(f32[256,15]{1,0:T(8,128)S(1)} %get-tuple-element.15), channel_id=1, source_target_pairs={{0,16},{16,32},{32,48},{48,64},{64,80},{80,96},{96,112},{1,17},{17... | collective-permute-start | bytes 46088 | tf_op jit(solution)/shard_map/ppermute | solution.py:49
  237.8 5.7 %collective-permute-start.3 = (f32[256,15]{1,0:T(8,128)S(1)}, f32[256,15]{1,0:T(8,128)S(1)}, u32[]{:S(2)}, u32[]{:S(2)}) collective-permute-start(f32[256,15]{1,0:T(8,128)S(1)} %get-tuple-element.16), channel_id=1, source_target_pairs={{16,0},{32,16},{48,32},{64,48},{80,64},{96,80},{112,96},{17,1},{33... | collective-permute-start | bytes 46088 | tf_op jit(solution)/shard_map/ppermute | solution.py:50
  243.6 9.9 %collective-permute-start.4 = (f32[15,542]{1,0:T(8,128)S(1)}, f32[15,542]{1,0:T(8,128)S(1)}, u32[]{:S(2)}, u32[]{:S(2)}) collective-permute-start(f32[15,542]{1,0:T(8,128)S(1)} %get-tuple-element.13), channel_id=1, source_target_pairs={{0,1},{1,2},{2,3},{3,4},{4,5},{5,6},{6,7},{7,8},{8,9},{9,10},{10,1... | collective-permute-start | bytes 97568 | tf_op jit(solution)/shard_map/ppermute | solution.py:49
  250.3 5.3 %collective-permute-start.5 = (f32[15,542]{1,0:T(8,128)S(1)}, f32[15,542]{1,0:T(8,128)S(1)}, u32[]{:S(2)}, u32[]{:S(2)}) collective-permute-start(f32[15,542]{1,0:T(8,128)S(1)} %get-tuple-element.14), channel_id=1, source_target_pairs={{1,0},{2,1},{3,2},{4,3},{5,4},{6,5},{7,6},{8,7},{9,8},{10,9},{11,1... | collective-permute-start | bytes 97568 | tf_op jit(solution)/shard_map/ppermute | solution.py:50
  326.0 11.6 %copy-start.1 = (f32[4,256,256]{2,1,0:T(8,128)S(1)}, f32[4,256,256]{2,1,0:T(8,128)}, u32[]{:S(2)}) copy-start(f32[4,256,256]{2,1,0:T(8,128)} %param.12) | copy-start | bytes 3145732
where the time goes:
time: 342 us; the launch traced here: 338 us
  blocking collectives  111 us (32%)
  local copies, waits for them, and re-layouts  71.7 us (21%)
  waiting for transfers between devices  54.5 us (16%)
  other arithmetic  34.5 us (10%)
  matrix products  34.1 us (10%)
  starting transfers between devices  31 us (9%)
    all_to_all x1, blocking collectives, shards(): lax.all_to_all(matched, 'epoch', split_axis=0, concat_axis=2, tiled=True)  56 us
    all_to_all x1, blocking collectives, side_by_side(): lax.all_to_all(both, axis, split_axis=split_dim, concat_axis=concat_dim,...  55.4 us
    all_to_all x2, waiting for transfers between devices, sum_at_owner(): tiles = lax.all_to_all(cut_along(value, dim, count), axis, 0, 0, tiled=True)  40.8 us
    gather x2, local copies, waits for them, and re-layouts, shards(): jnp.take(warped.reshape(tiles_dev * tile_rows, tile_cols), source, axis=0)  30.1 us
    ppermute x2, starting transfers between devices, padded_2(): before = lax.ppermute(last, axis, up)  17.1 us
    dot_general x1, matrix products, shards(): jnp.einsum('tik,tlk->til', half_warped, jnp.take(col_interp, tile_kinds,...  15.8 us
    all_to_all x2, starting transfers between devices, sum_at_owner(): tiles = lax.all_to_all(cut_along(value, dim, count), axis, 0, 0, tiled=True)  9.73 us
    gather x1, local copies, waits for them, and re-layouts, shards(): jnp.take(col_interp, tile_kinds, axis=0)  8.96 us
  transfers between devices with their start and end apart: 8, of which 6 were waited for; matrix products, arithmetic and copies ran while one was open for 4% of the time, Pallas kernels for 0%

commit v1 on v0

v1 whole, which is shorter than its diff:
```python
import functools

import jax
import jax.numpy as jnp
from jax import lax
from jax.experimental import pallas as pl
from jax.experimental.pallas import tpu as pltpu
from jax.sharding import PartitionSpec as P

F32 = jnp.float32
BF16 = jnp.bfloat16
MESH = pl.DeviceIdType.MESH
TILES_DEV = 12
PER_COL = 24
LOCAL_ROWS = 3328
SPAN = 3072
MIB = 2**20


def split_hi_lo(value):
    hi = value.astype(BF16)
    lo = (value - hi.astype(F32)).astype(BF16)
    return hi, lo


def dot(a, b):
    return jnp.dot(a, b, preferred_element_type=F32)


def dot_t(a, b):
    return lax.dot_general(a, b, (((1,), (1,)), ((), ())), preferred_element_type=F32)


def warp_kernel(
    kinds, heights, invvar, x_ref, r_ref, c_ref, placed, wrows, r_hi, r_lo, c_hi, c_lo, tops
):
    t = pl.program_id(0)
    strip = lax.axis_index("strip")
    block, side = strip // 2, strip % 2

    @pl.when(t == 0)
    def _():
        for k in range(4):
            r_hi[k], r_lo[k] = split_hi_lo(r_ref[k])
            c_hi[k], c_lo[k] = split_hi_lo(c_ref[k])
        placed[...] = jnp.zeros_like(placed)

        def above(i, top):
            @pl.when(i >= side * TILES_DEV)
            def _():
                tops[i - side * TILES_DEV] = top

            return top + heights[0, block, i]

        lax.fori_loop(0, (side + 1) * TILES_DEV, above, jnp.int32(0))
        row = lax.broadcasted_iota(jnp.int32, (32, 128), 0) * 128
        row = row + lax.broadcasted_iota(jnp.int32, (32, 128), 1)

        def weigh(i, acc):
            top = tops[i]
            live = (row >= top) & (row < top + heights[0, block, side * TILES_DEV + i])
            return jnp.where(live, invvar[0, i], acc)

        wrows[...] = lax.fori_loop(0, TILES_DEV, weigh, jnp.zeros((32, 128), F32))

    kind = kinds[0, t]
    height = heights[0, block, side * TILES_DEV + t]
    top = tops[t] - side * 1024
    live = lax.broadcasted_iota(jnp.int32, (256, 512), 0) < height
    x_hi, x_lo = split_hi_lo(jnp.where(live, x_ref[0, 0], 0.0))
    y = dot_t(x_hi, c_hi[kind]) + (dot_t(x_hi, c_lo[kind]) + dot_t(x_lo, c_hi[kind]))
    y_hi, y_lo = split_hi_lo(y)
    w = dot(r_hi[kind], y_hi) + (dot(r_hi[kind], y_lo) + dot(r_lo[kind], y_hi))
    w = jnp.where(live, w, 0.0)
    for p in range(4):
        placed[p, pl.ds(top, 256), :] = w[:, p * 128 : (p + 1) * 128]


def warp(raw_tiles, tile_kind, tile_invvar, tile_heights, row_interp, col_interp):
    smem = pl.BlockSpec(memory_space=pltpu.SMEM)
    whole = lambda shape: pl.BlockSpec(shape, lambda t: (0,) * len(shape))
    return pl.pallas_call(
        warp_kernel,
        grid=(TILES_DEV,),
        out_shape=(
            jax.ShapeDtypeStruct((4, LOCAL_ROWS, 128), F32),
            jax.ShapeDtypeStruct((32, 128), F32),
        ),
        in_specs=[
            smem,
            smem,
            smem,
            pl.BlockSpec((1, 1, 256, 512), lambda t: (0, t, 0, 0)),
            whole((4, 256, 256)),
            whole((4, 512, 512)),
        ],
        out_specs=(whole((4, LOCAL_ROWS, 128)), whole((32, 128))),
        scratch_shapes=[
            pltpu.VMEM((4, 256, 256), BF16),
            pltpu.VMEM((4, 256, 256), BF16),
            pltpu.VMEM((4, 512, 512), BF16),
            pltpu.VMEM((4, 512, 512), BF16),
            pltpu.SMEM((TILES_DEV,), jnp.int32),
        ],
        compiler_params=pltpu.CompilerParams(
            dimension_semantics=("arbitrary",), vmem_limit_bytes=48 * MIB
        ),
        name="warp",
    )(tile_kind, tile_heights, tile_invvar, raw_tiles, row_interp, col_interp)


def exchange_kernel(
    placed, wrows, sci, t_out, kept, prec, pb, wn, wbuf, sbuf, rbuf, zr, tt, tb,
    kept_sem, w_s, w_r, pair_s, pair_r, sci_s, sci_r, rs_s, rs_r, z_s, z_r,
    rel_s, rel_r, ag_s, ag_r, halo_s, halo_r, out_sem,
):
    e, s = lax.axis_index("epoch"), lax.axis_index("strip")
    zl, x = e // 4, e % 4
    c = s % 2
    pair = s + 1 - 2 * c
    q = 2 * x + zl
    x_right, x_left = zl * 4 + (x + 1) % 4, zl * 4 + (x + 3) % 4
    z_mate = (1 - zl) * 4 + x

    def send(src, dst, s_sem, r_sem, epoch, strip):
        copy = pltpu.make_async_remote_copy(
            src_ref=src, dst_ref=dst, send_sem=s_sem, recv_sem=r_sem,
            device_id={"epoch": epoch, "strip": strip}, device_id_type=MESH,
        )
        copy.start()

    def wait_on(ref, sem):
        pltpu.make_async_copy(ref, ref, sem).wait()

    def slab(ref, piece):
        return ref.at[:, pl.ds(piece * 256, 256), :]

    barrier = pltpu.get_barrier_semaphore()

    def greet(epoch, strip):
        pl.semaphore_signal(
            barrier, inc=1, device_id={"epoch": epoch, "strip": strip}, device_id_type=MESH
        )

    tb[:, 0:16, :] = jnp.zeros((32, 16, 128), F32)
    tb[:, 272:288, :] = jnp.zeros((32, 16, 128), F32)
    for k in range(1, 16):
        greet(e, (s + k) % 16)
    for k in range(1, 8):
        greet((e + k) % 8, s)
        greet((e + k) % 8, pair)
    for i in range(12):
        pltpu.make_async_copy(
            placed.at[pl.ds(2 * c, 2), pl.ds(i * 256, 256), :], slab(kept, i), kept_sem.at[i]
        ).start()
    pl.semaphore_wait(barrier, 29)

    for k in range(1, 16):
        epoch = (e + k % 8) % 8
        strip = s if k < 8 else pair
        send(wrows, wbuf.at[15 - k], w_s.at[k - 1], w_r.at[15 - k], epoch, strip)

    def piece_at(k):
        return (s // 2 + k // 2) % 8 * 2 + k % 2

    @pl.loop(0, 16)
    def _(k):
        i = piece_at(k) - 4 * c

        @pl.when((i >= 0) & (i < 12))
        def _():
            send(
                placed.at[pl.ds(2 * (1 - c), 2), pl.ds(i * 256, 256), :],
                slab(prec, i), pair_s.at[i], pair_r.at[i], e, pair,
            )

    for k in range(1, 16):
        wait_on(wbuf.at[15 - k], w_r.at[15 - k])
    mine = wrows[...] + wbuf[15 - 8]
    total = mine
    for k in range(1, 8):
        total = total + (wbuf[15 - k] + wbuf[15 - 8 - k])
    wbuf[15] = mine / total

    @pl.loop(0, 32)
    def _(i):
        row = jnp.broadcast_to(wbuf[15, pl.ds(i, 1), :], (128, 128))
        wn[pl.ds(i * 128, 128), :] = row.T

    def weighted(g, at):
        parts = []
        for j in range(2):
            rows = pl.ds((2 * g + j) * 256 + at * 64, 64)
            parts.append(pb[:, rows, :] * wn[rows, :][None])
        return parts

    def group_at(k):
        return (s // 2 + k) % 8

    def step_of(g):
        return 1 - 2 * (g % 2)

    @pl.loop(0, 8)
    def _(k):
        g = group_at(k)
        for j in range(2):
            r = 2 * g + j
            own, theirs = r - 4 * c, r - 4 * (1 - c)
            has_own = (own >= 0) & (own < 12)
            has_theirs = (theirs >= 0) & (theirs < 12)

            @pl.when(has_own)
            def _():
                wait_on(slab(kept, own), kept_sem.at[own])

            @pl.when(has_theirs)
            def _():
                wait_on(slab(prec, theirs), pair_r.at[theirs])

            @pl.when(has_own & has_theirs)
            def _():
                slab(pb, r)[...] = slab(kept, own)[...] + slab(prec, theirs)[...]

            @pl.when(has_own & jnp.logical_not(has_theirs))
            def _():
                slab(pb, r)[...] = slab(kept, own)[...]

            @pl.when(has_theirs & jnp.logical_not(has_own))
            def _():
                slab(pb, r)[...] = slab(prec, theirs)[...]

        step = step_of(g)
        parts = weighted(g, (x - step + 4) % 4)
        for j in range(2):
            sbuf[g, j] = parts[j]
        send(
            sbuf.at[g], rbuf.at[g, 0], rs_s.at[g], rs_r.at[g],
            zl * 4 + (x + step + 4) % 4, s,
        )
        for j in range(2):
            r = 2 * g + j

            @pl.when(r != s)
            def _():
                send(
                    slab(pb, r), sci.at[pl.ds(2 * s, 2)], sci_s.at[r], sci_r.at[s], e, r
                )

            @pl.when(r == s)
            def _():
                pltpu.make_async_copy(
                    slab(pb, r), sci.at[pl.ds(2 * s, 2)], sci_r.at[s]
                ).start()

    @pl.loop(0, 24)
    def _(m):
        k, g = m // 8, group_at(m % 8)
        step = step_of(g)
        wait_on(rbuf.at[g, k], rs_r.at[k * 8 + g])
        parts = weighted(g, (x - step * (2 + k) + 12) % 4)
        for j in range(2):
            rbuf[g, k, j] = rbuf[g, k, j] + parts[j]

        @pl.when(k < 2)
        def _():
            send(
                rbuf.at[g, k], rbuf.at[g, k + 1], rs_s.at[(k + 1) * 8 + g],
                rs_r.at[(k + 1) * 8 + g], zl * 4 + (x + step + 4) % 4, s,
            )

        @pl.when(k == 2)
        def _():
            send(
                rbuf.at[g, 2, :, :, pl.ds(32 * (1 - zl), 32), :], zr.at[g],
                z_s.at[g], z_r.at[g], z_mate, s,
            )

    @pl.loop(0, 8)
    def _(k):
        g = group_at(k)
        wait_on(zr.at[g], z_r.at[g])
        for j in range(2):
            r = 2 * g + j
            tt[r] = rbuf[g, 2, j, :, pl.ds(32 * zl, 32), :] + zr[g, j]
            there = tb.at[pl.ds(2 * s, 2), pl.ds(16 + 32 * q, 32), :]

            @pl.when(r != s)
            def _():
                send(tt.at[r], there, rel_s.at[r], rel_r.at[s], e, r)

            @pl.when(r == s)
            def _():
                pltpu.make_async_copy(tt.at[r], there, rel_r.at[s]).start()

    def seg(j, first, count):
        return tb.at[pl.ds(8 * j, 8), pl.ds(16 + first, count), :]

    own_rows, mate_rows = 32 * q, 32 * (2 * x + 1 - zl)

    @pl.loop(0, 4)
    def _(j):
        for i in range(4):
            source = 4 * j + i
            wait_on(
                tb.at[pl.ds(2 * source, 2), pl.ds(16 + 32 * q, 32), :], rel_r.at[source]
            )
        part = seg(j, own_rows, 32)
        send(part, part, ag_s.at[j], ag_r.at[j], z_mate, s)
        send(part, part, ag_s.at[4 + j], ag_r.at[4 + j], x_right, s)
        send(part, part, ag_s.at[8 + j], ag_r.at[8 + j], x_left, s)

    @pl.loop(0, 4)
    def _(j):
        part = seg(j, mate_rows, 32)
        wait_on(part, ag_r.at[j])
        send(part, part, ag_s.at[12 + j], ag_r.at[12 + j], x_right, s)
        send(part, part, ag_s.at[16 + j], ag_r.at[16 + j], x_left, s)

    @pl.loop(0, 4)
    def _(j):
        left, right = (x + 3) % 4, (x + 1) % 4
        wait_on(seg(j, 64 * left + 32 * zl, 32), ag_r.at[4 + j])
        wait_on(seg(j, 64 * left + 32 * (1 - zl), 32), ag_r.at[12 + j])
        wait_on(seg(j, 64 * right + 32 * zl, 32), ag_r.at[8 + j])
        wait_on(seg(j, 64 * right + 32 * (1 - zl), 32), ag_r.at[16 + j])

        @pl.when(j % 2 == 0)
        def _():
            part = seg(j, 64 * left, 64)
            send(part, part, ag_s.at[20 + j], ag_r.at[20 + j], x_right, s)

        @pl.when(j % 2 == 1)
        def _():
            part = seg(j, 64 * right, 64)
            send(part, part, ag_s.at[20 + j], ag_r.at[20 + j], x_left, s)

    @pl.loop(0, 4)
    def _(j):
        wait_on(seg(j, 64 * ((x + 2) % 4), 64), ag_r.at[20 + j])
        planes = pl.ds(8 * j, 8)

        @pl.when(s > 0)
        def _():
            send(
                tb.at[planes, 16:32, :], tb.at[planes, 272:288, :],
                halo_s.at[j], halo_r.at[j], e, s - 1,
            )

        @pl.when(s < 15)
        def _():
            send(
                tb.at[planes, 256:272, :], tb.at[planes, 0:16, :],
                halo_s.at[4 + j], halo_r.at[4 + j], e, s + 1,
            )

    @pl.loop(0, 4)
    def _(j):
        planes = pl.ds(8 * j, 8)

        @pl.when(s < 15)
        def _():
            wait_on(tb.at[planes, 272:288, :], halo_r.at[j])

        @pl.when(s > 0)
        def _():
            wait_on(tb.at[planes, 0:16, :], halo_r.at[4 + j])

        pltpu.make_async_copy(tb.at[planes], t_out.at[planes], out_sem.at[j]).start()

    for i in range(4):
        wait_on(tb.at[pl.ds(8 * i, 8)], out_sem.at[i])
    for k in range(15):
        wait_on(wrows, w_s.at[k])

    @pl.loop(0, 12)
    def _(i):
        wait_on(slab(prec, i), pair_s.at[i])

    @pl.loop(0, 16)
    def _(r):
        wait_on(sci.at[pl.ds(2 * r, 2)], sci_r.at[r])

        @pl.when(r != s)
        def _():
            wait_on(slab(pb, r), sci_s.at[r])
            wait_on(tt.at[r], rel_s.at[r])

    @pl.loop(0, 24)
    def _(m):
        wait_on(sbuf.at[0], rs_s.at[m])

    @pl.loop(0, 8)
    def _(g):
        wait_on(zr.at[g], z_s.at[g])

    @pl.loop(0, 20)
    def _(m):
        wait_on(seg(0, 0, 32), ag_s.at[m])

    @pl.loop(0, 4)
    def _(j):
        wait_on(seg(0, 0, 64), ag_s.at[20 + j])

        @pl.when(s > 0)
        def _():
            wait_on(tb.at[0:8, 0:16, :], halo_s.at[j])

        @pl.when(s < 15)
        def _():
            wait_on(tb.at[0:8, 0:16, :], halo_s.at[4 + j])


def exchange(placed, wrows):
    vmem = lambda *shape: pltpu.VMEM(shape, F32)
    dma = lambda count: pltpu.SemaphoreType.DMA((count,))
    return pl.pallas_call(
        exchange_kernel,
        out_shape=(
            jax.ShapeDtypeStruct((32, 256, 128), F32),
            jax.ShapeDtypeStruct((32, 288, 128), F32),
        ),
        in_specs=[
            pl.BlockSpec(memory_space=pl.ANY),
            pl.BlockSpec(memory_space=pltpu.VMEM),
        ],
        out_specs=(pl.BlockSpec(memory_space=pl.ANY), pl.BlockSpec(memory_space=pl.ANY)),
        scratch_shapes=[
            vmem(2, SPAN, 128),
            vmem(2, SPAN, 128),
            vmem(2, 4096, 128),
            vmem(4096, 128),
            vmem(16, 32, 128),
            vmem(8, 2, 2, 64, 128),
            vmem(8, 3, 2, 2, 64, 128),
            vmem(8, 2, 2, 32, 128),
            vmem(16, 2, 32, 128),
            vmem(32, 288, 128),
            dma(12),
            dma(15), dma(15),
            dma(12), dma(12),
            dma(16), dma(16),
            dma(24), dma(24),
            dma(8), dma(8),
            dma(16), dma(16),
            dma(24), dma(24),
            dma(8), dma(8),
            dma(4),
        ],
        compiler_params=pltpu.CompilerParams(
            collective_id=0, has_side_effects=True, vmem_limit_bytes=40 * MIB
        ),
        name="exchange",
    )(placed, wrows)


def match_kernel(prof, poly, main, before, after, sci, out, band, toep):
    j = pl.program_id(0)
    steps = pl.num_programs(0)
    e, s = lax.axis_index("epoch"), lax.axis_index("strip")

    def taps(offset, k, axis):
        def add(i, acc):
            return jnp.where(offset == i, prof[k, axis, i], acc)

        return lax.fori_loop(0, 31, add, jnp.zeros(offset.shape, F32), unroll=True)

    @pl.when(j == 0)
    def _():
        lane = lax.broadcasted_iota(jnp.int32, (128, 480), 1)
        section = (lane >= 160).astype(jnp.int32) + (lane >= 320).astype(jnp.int32)
        offset = lane - 160 * section - lax.broadcasted_iota(jnp.int32, (128, 480), 0) - 1
        for k in range(2):
            hi, lo = split_hi_lo(taps(offset, k, 0))
            band[128 * k : 128 * k + 128, :] = jnp.where(
                section == 1, lo.astype(F32), hi.astype(F32)
            ).astype(BF16)
        m = lax.broadcasted_iota(jnp.int32, (256, 128), 0)
        source = jnp.where(m < 192, m, m - 256)
        offset = source - lax.broadcasted_iota(jnp.int32, (256, 128), 1) + 15
        for k in range(2):
            hi, lo = split_hi_lo(taps(offset, k, 1))
            toep[k, :, 0:128] = hi
            toep[k, :, 128:256] = lo

    planes = [jnp.where(j > 0, before[0], 0.0)] + [main[p] for p in range(8)]
    planes.append(jnp.where(j < steps - 1, after[0], 0.0))
    rows = []
    t_hi, t_lo = split_hi_lo(jnp.concatenate(planes, axis=1))
    for half in range(2):
        at = slice(128 * half, 128 * half + 160)
        stacked = jnp.concatenate([t_hi[at], t_hi[at], t_lo[at]], axis=0)
        rows.append(dot(band[...], stacked))
    lane = lax.broadcasted_iota(jnp.int32, (256, 128), 1)
    conv = []
    for k in range(2):
        both = jnp.concatenate([part[128 * k : 128 * k + 128] for part in rows], axis=0)
        cut = [both[:, 128 * p : 128 * p + 128] for p in range(10)]
        inputs = [
            jnp.concatenate([cut[p], jnp.where(lane < 64, cut[p + 1], cut[p - 1])], axis=1)
            for p in range(1, 9)
        ]
        hi, lo = split_hi_lo(jnp.concatenate(inputs, axis=0))
        first = dot(hi, toep[k])
        conv.append(first[:, :128] + (first[:, 128:] + dot(lo, toep[k, :, 0:128])))
    row = lax.broadcasted_iota(jnp.int32, (256, 128), 0) + s * 256
    u = (2.0 * row.astype(F32) + 1.0) / 4096.0 - 1.0
    terms = [[poly[e, k, i] for i in range(6)] for k in range(2)]
    base = [t[0] + t[1] * u + t[3] * u * u for t in terms]
    slope = [t[2] + t[4] * u for t in terms]
    for p in range(8):
        col = lane + (j * 8 + p) * 128
        v = (2.0 * col.astype(F32) + 1.0) / 4096.0 - 1.0
        at = slice(256 * p, 256 * p + 256)
        coeff = [base[k] + v * (slope[k] + terms[k][5] * v) for k in range(2)]
        out[0, :, 128 * p : 128 * p + 128] = sci[p] - (
            coeff[0] * conv[0][at] + coeff[1] * conv[1][at]
        )


def match(profiles, poly, template, science):
    smem = pl.BlockSpec(memory_space=pltpu.SMEM)
    return pl.pallas_call(
        match_kernel,
        grid=(4,),
        out_shape=jax.ShapeDtypeStruct((1, 256, 4096), F32),
        in_specs=[
            smem,
            smem,
            pl.BlockSpec((8, 288, 128), lambda j: (j, 0, 0)),
            pl.BlockSpec((1, 288, 128), lambda j: (jnp.maximum(8 * j - 1, 0), 0, 0)),
            pl.BlockSpec((1, 288, 128), lambda j: (jnp.minimum(8 * j + 8, 31), 0, 0)),
            pl.BlockSpec((8, 256, 128), lambda j: (j, 0, 0)),
        ],
        out_specs=pl.BlockSpec((1, 256, 1024), lambda j: (0, 0, j)),
        scratch_shapes=[pltpu.VMEM((256, 480), BF16), pltpu.VMEM((2, 256, 256), BF16)],
        compiler_params=pltpu.CompilerParams(
            dimension_semantics=("arbitrary",), vmem_limit_bytes=48 * MIB
        ),
        name="match",
    )(profiles, poly, template, template, template, science)


def shards(
    raw_tiles, tile_kind, tile_invvar, tile_heights, row_interp, col_interp, psf_profiles, psf_poly
):
    placed, wrows = warp(
        raw_tiles, tile_kind, tile_invvar, tile_heights, row_interp, col_interp
    )
    science, template = exchange(placed, wrows)
    return match(psf_profiles, psf_poly, template, science)


def solution(mesh):
    in_specs = (
        P("epoch", "strip", None, None),
        P("epoch", "strip"),
        P("epoch", "strip"),
        P("epoch", None, None),
        P(),
        P(),
        P(),
        P(),
    )
    out_specs = P("epoch", "strip", None)
    return jax.shard_map(shards, mesh=mesh, in_specs=in_specs, out_specs=out_specs, check_vma=False)
```

time: 342 us -> 178 us (0.52)
  the two profiles are of different devices: /device:TPU:81 before, /device:TPU:1 now
where the time goes in v1:
time: 178 us
  Pallas kernels  166 us (93%)
  local copies, waits for them, and re-layouts  11.8 us (7%)
    pallas_call x1, Pallas kernels, exchange(): pl.pallas_call(exchange_kernel, out_shape=(jax.ShapeDtypeStruct((32, 256,...  135 us
    pallas_call x1, Pallas kernels, warp(): pl.pallas_call(warp_kernel, grid=(TILES_DEV,), out_shape=(jax.ShapeDtypeS...  17.7 us
    pallas_call x1, Pallas kernels, match(): pl.pallas_call(match_kernel, grid=(4,), out_shape=jax.ShapeDtypeStruct((1...  13.4 us
    unnamed x21, local copies, waits for them, and re-layouts  11.8 us

profile of v1, /device:TPU:1, one launch (start us, length us, event | category | flops | bytes accessed | tf_op | source)
XLA Modules:
  0.0 177.9 jit_solution(810678606141198298)
XLA Ops:
  0.0 0.0 copy-start.1
  0.0 2.2 %copy-done.1 = f32[4,512,512]{2,1,0:T(8,128)S(1)} copy-done((f32[4,512,512]{2,1,0:T(8,128)S(1)}, f32[4,512,512]{2,1,0:T(8,128)}, u32[]{:S(2)}) %copy-start.1) | copy-done | bytes 4194328
  2.2 0.0 copy-start.4
  2.2 1.2 copy-done.4
  3.4 0.0 copy-start.5
  3.4 0.7 copy-done.5
  4.1 0.0 copy-start.7
  4.1 0.7 copy-done.7
  4.8 0.0 copy-start.8
  4.8 0.7 copy-done.8
  5.4 17.7 %warp.1 = (f32[4,3328,128]{2,1,0:T(8,128)}, f32[32,128]{1,0:T(8,128)S(1)}) custom-call(s32[1,12]{1,0:T(1,128)S(1)} %copy-done.7, s32[1,8,24]{2,1,0:T(8,128)S(1)} %copy-done.5, f32[1,12]{1,0:T(1,128)S(1)} %copy-done.8, f32[1,12,256,512]{3,2,1,0:T(8,128)} %x_ref.1, f32[4,256,256]{2,1,0:T(8,128)S(1)} %copy-done.4, f32[4,512,512]{2,1,0:T(8,128)S(1)} %copy-done.1), custom_call_target="tpu_custom_call" | custom-call | tf_op jit(solution)/shard_map/warp/pallas_call | solution.py:82
  23.1 0.0 copy-start.9
  23.1 0.0 copy-start.6
  23.1 134.9 %exchange.1 = (f32[32,256,128]{2,1,0:T(8,128)S(1)}, f32[32,288,128]{2,1,0:T(8,128)S(1)}) custom-call(f32[4,3328,128]{2,1,0:T(8,128)} %get-tuple-element.9.placed, f32[32,128]{1,0:T(8,128)S(1)} %get-tuple-element.10.wrows), custom_call_target="tpu_custom_call" | custom-call | tf_op jit(solution)/shard_map/exchange/pallas_call | solution.py:416
  158.0 0.0 copy-start
  158.0 2.1 %copy-done = f32[32,288,128]{2,1,0:T(8,128)} copy-done((f32[32,288,128]{2,1,0:T(8,128)}, f32[32,288,128]{2,1,0:T(8,128)S(1)}, u32[]{:S(2)}) %copy-start) | copy-done | bytes 4718616
  160.1 0.0 copy-start.2
  160.1 2.0 %copy-done.2 = f32[32,256,128]{2,1,0:T(8,128)} copy-done((f32[32,256,128]{2,1,0:T(8,128)}, f32[32,256,128]{2,1,0:T(8,128)S(1)}, u32[]{:S(2)}) %copy-start.2) | copy-done | bytes 4194328
  162.2 0.0 copy-done.9
  162.2 0.1 copy.9.poly
  162.2 0.0 copy-done.6
  162.3 0.0 copy-start.3
  162.3 2.2 %copy-done.3 = f32[32,256,128]{2,1,0:T(8,128)S(1)} copy-done((f32[32,256,128]{2,1,0:T(8,128)S(1)}, f32[32,256,128]{2,1,0:T(8,128)}, u32[]{:S(2)}) %copy-start.3) | copy-done | bytes 4194328
  164.4 13.4 %match.1 = f32[1,256,4096]{2,1,0:T(8,128)} custom-call(f32[2,2,31]{2,1,0:T(2,128)S(1)} %copy-done.6, f32[8,2,6]{2,1,0:T(2,128)S(1)} %copy.9.poly, f32[32,288,128]{2,1,0:T(8,128)} %copy-done, f32[32,288,128]{2,1,0:T(8,128)} %copy-done, f32[32,288,128]{2,1,0:T(8,128)} %copy-done, f32[32,256,128]{2,1,0:T(8,128)S(1)} %copy-done.3), custom_call_target="tpu_custom_call" | custom-call | tf_op jit(solution)/shard_map/match/pallas_call | solution.py:522
Async XLA Ops:
  0.0 2.2 %copy-start.1 = (f32[4,512,512]{2,1,0:T(8,128)S(1)}, f32[4,512,512]{2,1,0:T(8,128)}, u32[]{:S(2)}) copy-start(f32[4,512,512]{2,1,0:T(8,128)} %c_ref.1) | copy-start | bytes 12582916
  2.2 1.2 copy-start.4
  3.4 0.7 copy-start.5
  4.1 0.7 copy-start.7
  4.8 0.7 copy-start.8
  23.1 139.1 %copy-start.9 = (f32[8,2,6]{0,1,2:T(2,128)S(1)}, f32[8,2,6]{0,1,2:T(2,128)}, u32[]{:S(2)}) copy-start(f32[8,2,6]{0,1,2:T(2,128)} %param.15) | copy-start | bytes 1156
  23.1 139.2 %copy-start.6 = (f32[2,2,31]{2,1,0:T(2,128)S(1)}, f32[2,2,31]{2,1,0:T(2,128)}, u32[]{:S(2)}) copy-start(f32[2,2,31]{2,1,0:T(2,128)} %prof.1) | copy-start | bytes 1492
  158.0 2.1 %copy-start = (f32[32,288,128]{2,1,0:T(8,128)}, f32[32,288,128]{2,1,0:T(8,128)S(1)}, u32[]{:S(2)}) copy-start(f32[32,288,128]{2,1,0:T(8,128)S(1)} %get-tuple-element.11.main.before.after) | copy-start | bytes 14155780
  160.1 2.0 %copy-start.2 = (f32[32,256,128]{2,1,0:T(8,128)}, f32[32,256,128]{2,1,0:T(8,128)S(1)}, u32[]{:S(2)}) copy-start(f32[32,256,128]{2,1,0:T(8,128)S(1)} %get-tuple-element.12.sci) | copy-start | bytes 12582916
  162.3 2.2 %copy-start.3 = (f32[32,256,128]{2,1,0:T(8,128)S(1)}, f32[32,256,128]{2,1,0:T(8,128)}, u32[]{:S(2)}) copy-start(f32[32,256,128]{2,1,0:T(8,128)} %copy-done.2) | copy-start | bytes 12582916

commit v2 on v1

--- a/solution.py
+++ b/solution.py
@@ -14,7 +14,15 @@
 PER_COL = 24
 LOCAL_ROWS = 3328
 SPAN = 3072
-MIB = 2**20
+VMEM_BYTES = 67043328
+ROW_SENDS = (
+    ((0, 0, 1), (1, 0, 0), (0, 1, 0), (0, 3, 0)),
+    ((1, 1, 0), (1, 3, 1)),
+    ((0, 2, 0),),
+    ((1, 2, 0), (0, 2, 1)),
+    ((1, 1, 1), (1, 3, 0)),
+    ((0, 1, 1), (0, 3, 1), (1, 0, 1), (1, 2, 1)),
+)
 
 
 def split_hi_lo(value):
@@ -103,14 +111,14 @@
             pltpu.SMEM((TILES_DEV,), jnp.int32),
         ],
         compiler_params=pltpu.CompilerParams(
-            dimension_semantics=("arbitrary",), vmem_limit_bytes=48 * MIB
+            dimension_semantics=("arbitrary",), vmem_limit_bytes=VMEM_BYTES
         ),
         name="warp",
     )(tile_kind, tile_heights, tile_invvar, raw_tiles, row_interp, col_interp)
 
 
 def exchange_kernel(
-    placed, wrows, sci, t_out, kept, prec, pb, wn, wbuf, sbuf, rbuf, zr, tt, tb,
+    placed, wrows, sci, t_out, kept, prec, pb, wn, wbuf, wi, sbuf, rbuf, zr, tt, tb,
     kept_sem, w_s, w_r, pair_s, pair_r, sci_s, sci_r, rs_s, rs_r, z_s, z_r,
     rel_s, rel_r, ag_s, ag_r, halo_s, halo_r, out_sem,
 ):
@@ -174,31 +182,33 @@
                 slab(prec, i), pair_s.at[i], pair_r.at[i], e, pair,
             )
 
-    for k in range(1, 16):
-        wait_on(wbuf.at[15 - k], w_r.at[15 - k])
-    mine = wrows[...] + wbuf[15 - 8]
-    total = mine
-    for k in range(1, 8):
-        total = total + (wbuf[15 - k] + wbuf[15 - 8 - k])
-    wbuf[15] = mine / total
+    wait_on(wbuf.at[7], w_r.at[7])
+    wbuf[15] = wrows[...] + wbuf[7]
 
     @pl.loop(0, 32)
     def _(i):
         row = jnp.broadcast_to(wbuf[15, pl.ds(i, 1), :], (128, 128))
         wn[pl.ds(i * 128, 128), :] = row.T
 
-    def weighted(g, at):
-        parts = []
-        for j in range(2):
-            rows = pl.ds((2 * g + j) * 256 + at * 64, 64)
-            parts.append(pb[:, rows, :] * wn[rows, :][None])
-        return parts
-
     def group_at(k):
         return (s // 2 + k) % 8
 
     def step_of(g):
         return 1 - 2 * (g % 2)
+
+    def weighted(h, g, j, at):
+        rows = pl.ds((2 * g + j) * 256 + at * 64, 64)
+        return pb[h, rows, :] * wn[rows, :]
+
+    def pass_on(src, h, g, k):
+        to = zl * 4 + (x + step_of(g) + 4) % 4
+        at = 24 * h + 8 * k + g
+        send(src, rbuf.at[h, g, k], rs_s.at[at], rs_r.at[at], to, s)
+
+    def begin(h, g):
+        for j in range(2):
+            sbuf[h, g, j] = weighted(h, g, j, (x - step_of(g) + 4) % 4)
+        pass_on(sbuf.at[h, g], h, g, 0)
 
     @pl.loop(0, 8)
     def _(k):
@@ -229,143 +239,161 @@
             def _():
                 slab(pb, r)[...] = slab(prec, theirs)[...]
 
-        step = step_of(g)
-        parts = weighted(g, (x - step + 4) % 4)
-        for j in range(2):
-            sbuf[g, j] = parts[j]
-        send(
-            sbuf.at[g], rbuf.at[g, 0], rs_s.at[g], rs_r.at[g],
-            zl * 4 + (x + step + 4) % 4, s,
-        )
-        for j in range(2):
-            r = 2 * g + j
-
-            @pl.when(r != s)
+        begin(0, g)
+
+    def send_rows(batch):
+        for dz, dy, dc in ROW_SENDS[batch]:
+            r = (s // 8 + dz) % 2 * 8 + (s // 2 + dy) % 4 * 2 + (c + dc) % 2
+            send(slab(pb, r), sci.at[pl.ds(2 * s, 2)], sci_s.at[r], sci_r.at[s], e, r)
+
+    def ring_step(h, k):
+        @pl.loop(0, 8)
+        def _(i):
+            g = group_at(i)
+            wait_on(rbuf.at[h, g, k], rs_r.at[24 * h + 8 * k + g])
+            at = (x - step_of(g) * (2 + k) + 12) % 4
+            for j in range(2):
+                rbuf[h, g, k, j] = rbuf[h, g, k, j] + weighted(h, g, j, at)
+            if k < 2:
+                pass_on(rbuf.at[h, g, k], h, g, k + 1)
+            else:
+                away = rbuf.at[h, g, 2, :, pl.ds(32 * (1 - zl), 32), :]
+                send(away, zr.at[h, g], z_s.at[8 * h + g], z_r.at[8 * h + g], z_mate, s)
+
+    def finish(h):
+        there = tb.at[16 * h + s, pl.ds(16 + 32 * q, 32), :]
+
+        @pl.loop(0, 8)
+        def _(k):
+            g = group_at(k)
+            wait_on(zr.at[h, g], z_r.at[8 * h + g])
+            for j in range(2):
+                r = 2 * g + j
+                inverse = wi[pl.ds(128 * r + 32 * (q % 4), 32), :]
+                summed = rbuf[h, g, 2, j, pl.ds(32 * zl, 32), :] + zr[h, g, j]
+                tt[h, r] = summed * inverse
+
+                @pl.when(r != s)
+                def _():
+                    send(tt.at[h, r], there, rel_s.at[16 * h + r], rel_r.at[16 * h + s], e, r)
+
+                @pl.when(r == s)
+                def _():
+                    pltpu.make_async_copy(tt.at[h, r], there, rel_r.at[16 * h + s]).start()
+
+    def seg(j, first, count):
+        return tb.at[pl.ds(8 * j, 8), pl.ds(16 + first, count), :]
+
+    own_rows, mate_rows = 32 * q, 32 * (2 * x + 1 - zl)
+    left, right = (x + 3) % 4, (x + 1) % 4
+
+    def gather_own(h):
+        for j in (2 * h, 2 * h + 1):
+            @pl.loop(8 * j, 8 * j + 8)
+            def _(i):
+                wait_on(tb.at[i, pl.ds(16 + 32 * q, 32), :], rel_r.at[i])
+
+            part = seg(j, own_rows, 32)
+            send(part, part, ag_s.at[j], ag_r.at[j], z_mate, s)
+            send(part, part, ag_s.at[4 + j], ag_r.at[4 + j], x_right, s)
+            send(part, part, ag_s.at[8 + j], ag_r.at[8 + j], x_left, s)
+
+    def gather_mate(h):
+        for j in (2 * h, 2 * h + 1):
+            part = seg(j, mate_rows, 32)
+            wait_on(part, ag_r.at[j])
+            send(part, part, ag_s.at[12 + j], ag_r.at[12 + j], x_right, s)
+            send(part, part, ag_s.at[16 + j], ag_r.at[16 + j], x_left, s)
+
+    def gather_far(h):
+        for j in (2 * h, 2 * h + 1):
+            wait_on(seg(j, 64 * left + 32 * zl, 32), ag_r.at[4 + j])
+            wait_on(seg(j, 64 * left + 32 * (1 - zl), 32), ag_r.at[12 + j])
+            wait_on(seg(j, 64 * right + 32 * zl, 32), ag_r.at[8 + j])
+            wait_on(seg(j, 64 * right + 32 * (1 - zl), 32), ag_r.at[16 + j])
+            if j % 2 == 0:
+                part = seg(j, 64 * left, 64)
+                send(part, part, ag_s.at[20 + j], ag_r.at[20 + j], x_right, s)
+            else:
+                part = seg(j, 64 * right, 64)
+                send(part, part, ag_s.at[20 + j], ag_r.at[20 + j], x_left, s)
+
+    def edges(h):
+        for j in (2 * h, 2 * h + 1):
+            wait_on(seg(j, 64 * ((x + 2) % 4), 64), ag_r.at[20 + j])
+            planes = pl.ds(8 * j, 8)
+
+            @pl.when(s > 0)
             def _():
                 send(
-                    slab(pb, r), sci.at[pl.ds(2 * s, 2)], sci_s.at[r], sci_r.at[s], e, r
+                    tb.at[planes, 16:32, :], tb.at[planes, 272:288, :],
+                    halo_s.at[j], halo_r.at[j], e, s - 1,
                 )
 
-            @pl.when(r == s)
-            def _():
-                pltpu.make_async_copy(
-                    slab(pb, r), sci.at[pl.ds(2 * s, 2)], sci_r.at[s]
-                ).start()
-
-    @pl.loop(0, 24)
-    def _(m):
-        k, g = m // 8, group_at(m % 8)
-        step = step_of(g)
-        wait_on(rbuf.at[g, k], rs_r.at[k * 8 + g])
-        parts = weighted(g, (x - step * (2 + k) + 12) % 4)
-        for j in range(2):
-            rbuf[g, k, j] = rbuf[g, k, j] + parts[j]
-
-        @pl.when(k < 2)
-        def _():
-            send(
-                rbuf.at[g, k], rbuf.at[g, k + 1], rs_s.at[(k + 1) * 8 + g],
-                rs_r.at[(k + 1) * 8 + g], zl * 4 + (x + step + 4) % 4, s,
-            )
-
-        @pl.when(k == 2)
-        def _():
-            send(
-                rbuf.at[g, 2, :, :, pl.ds(32 * (1 - zl), 32), :], zr.at[g],
-                z_s.at[g], z_r.at[g], z_mate, s,
-            )
+            @pl.when(s < 15)
+            def _():
+                send(
+                    tb.at[planes, 256:272, :], tb.at[planes, 0:16, :],
+                    halo_s.at[4 + j], halo_r.at[4 + j], e, s + 1,
+                )
+
+    def leave(h):
+        for j in (2 * h, 2 * h + 1):
+            planes = pl.ds(8 * j, 8)
+
+            @pl.when(s < 15)
+            def _():
+                wait_on(tb.at[planes, 272:288, :], halo_r.at[j])
+
+            @pl.when(s > 0)
+            def _():
+                wait_on(tb.at[planes, 0:16, :], halo_r.at[4 + j])
+
+            pltpu.make_async_copy(tb.at[planes], t_out.at[planes], out_sem.at[j]).start()
+
+    send_rows(0)
+    pltpu.make_async_copy(slab(pb, s), sci.at[pl.ds(2 * s, 2)], sci_r.at[s]).start()
+    ring_step(0, 0)
+    send_rows(1)
+    ring_step(0, 1)
 
     @pl.loop(0, 8)
     def _(k):
-        g = group_at(k)
-        wait_on(zr.at[g], z_r.at[g])
-        for j in range(2):
-            r = 2 * g + j
-            tt[r] = rbuf[g, 2, j, :, pl.ds(32 * zl, 32), :] + zr[g, j]
-            there = tb.at[pl.ds(2 * s, 2), pl.ds(16 + 32 * q, 32), :]
-
-            @pl.when(r != s)
-            def _():
-                send(tt.at[r], there, rel_s.at[r], rel_r.at[s], e, r)
-
-            @pl.when(r == s)
-            def _():
-                pltpu.make_async_copy(tt.at[r], there, rel_r.at[s]).start()
-
-    def seg(j, first, count):
-        return tb.at[pl.ds(8 * j, 8), pl.ds(16 + first, count), :]
-
-    own_rows, mate_rows = 32 * q, 32 * (2 * x + 1 - zl)
-
-    @pl.loop(0, 4)
-    def _(j):
-        for i in range(4):
-            source = 4 * j + i
-            wait_on(
-                tb.at[pl.ds(2 * source, 2), pl.ds(16 + 32 * q, 32), :], rel_r.at[source]
-            )
-        part = seg(j, own_rows, 32)
-        send(part, part, ag_s.at[j], ag_r.at[j], z_mate, s)
-        send(part, part, ag_s.at[4 + j], ag_r.at[4 + j], x_right, s)
-        send(part, part, ag_s.at[8 + j], ag_r.at[8 + j], x_left, s)
-
-    @pl.loop(0, 4)
-    def _(j):
-        part = seg(j, mate_rows, 32)
-        wait_on(part, ag_r.at[j])
-        send(part, part, ag_s.at[12 + j], ag_r.at[12 + j], x_right, s)
-        send(part, part, ag_s.at[16 + j], ag_r.at[16 + j], x_left, s)
-
-    @pl.loop(0, 4)
-    def _(j):
-        left, right = (x + 3) % 4, (x + 1) % 4
-        wait_on(seg(j, 64 * left + 32 * zl, 32), ag_r.at[4 + j])
-        wait_on(seg(j, 64 * left + 32 * (1 - zl), 32), ag_r.at[12 + j])
-        wait_on(seg(j, 64 * right + 32 * zl, 32), ag_r.at[8 + j])
-        wait_on(seg(j, 64 * right + 32 * (1 - zl), 32), ag_r.at[16 + j])
-
-        @pl.when(j % 2 == 0)
-        def _():
-            part = seg(j, 64 * left, 64)
-            send(part, part, ag_s.at[20 + j], ag_r.at[20 + j], x_right, s)
-
-        @pl.when(j % 2 == 1)
-        def _():
-            part = seg(j, 64 * right, 64)
-            send(part, part, ag_s.at[20 + j], ag_r.at[20 + j], x_left, s)
-
-    @pl.loop(0, 4)
-    def _(j):
-        wait_on(seg(j, 64 * ((x + 2) % 4), 64), ag_r.at[20 + j])
-        planes = pl.ds(8 * j, 8)
-
-        @pl.when(s > 0)
-        def _():
-            send(
-                tb.at[planes, 16:32, :], tb.at[planes, 272:288, :],
-                halo_s.at[j], halo_r.at[j], e, s - 1,
-            )
-
-        @pl.when(s < 15)
-        def _():
-            send(
-                tb.at[planes, 256:272, :], tb.at[planes, 0:16, :],
-                halo_s.at[4 + j], halo_r.at[4 + j], e, s + 1,
-            )
-
-    @pl.loop(0, 4)
-    def _(j):
-        planes = pl.ds(8 * j, 8)
-
-        @pl.when(s < 15)
-        def _():
-            wait_on(tb.at[planes, 272:288, :], halo_r.at[j])
-
-        @pl.when(s > 0)
-        def _():
-            wait_on(tb.at[planes, 0:16, :], halo_r.at[4 + j])
-
-        pltpu.make_async_copy(tb.at[planes], t_out.at[planes], out_sem.at[j]).start()
+        begin(1, group_at(k))
+
+    send_rows(2)
+    for k in range(1, 16):
+        if k != 8:
+            wait_on(wbuf.at[15 - k], w_r.at[15 - k])
+    total = wbuf[15]
+    for k in range(1, 8):
+        total = total + (wbuf[15 - k] + wbuf[15 - 8 - k])
+    wbuf[15] = 1.0 / total
+
+    @pl.loop(0, 16)
+    def _(r):
+        row = jnp.broadcast_to(wbuf[15, pl.ds(2 * r + q // 4, 1), :], (128, 128))
+        wi[pl.ds(128 * r, 128), :] = row.T
+
+    ring_step(0, 2)
+    send_rows(3)
+    ring_step(1, 0)
+    finish(0)
+    send_rows(4)
+    ring_step(1, 1)
+    gather_own(0)
+    ring_step(1, 2)
+    gather_mate(0)
+    finish(1)
+    gather_far(0)
+    gather_own(1)
+    send_rows(5)
+    gather_mate(1)
+    edges(0)
+    gather_far(1)
+    leave(0)
+    edges(1)
+    leave(1)
 
     for i in range(4):
         wait_on(tb.at[pl.ds(8 * i, 8)], out_sem.at[i])
@@ -383,15 +411,16 @@
         @pl.when(r != s)
         def _():
             wait_on(slab(pb, r), sci_s.at[r])
-            wait_on(tt.at[r], rel_s.at[r])
-
-    @pl.loop(0, 24)
+            wait_on(tt.at[0, r], rel_s.at[r])
+            wait_on(tt.at[1, r], rel_s.at[16 + r])
+
+    @pl.loop(0, 48)
     def _(m):
-        wait_on(sbuf.at[0], rs_s.at[m])
-
-    @pl.loop(0, 8)
+        wait_on(sbuf.at[0, 0], rs_s.at[m])
+
+    @pl.loop(0, 16)
     def _(g):
-        wait_on(zr.at[g], z_s.at[g])
+        wait_on(zr.at[0, 0], z_s.at[g])
 
     @pl.loop(0, 20)
     def _(m):
@@ -430,30 +459,31 @@
             vmem(2, 4096, 128),
             vmem(4096, 128),
             vmem(16, 32, 128),
-            vmem(8, 2, 2, 64, 128),
-            vmem(8, 3, 2, 2, 64, 128),
-            vmem(8, 2, 2, 32, 128),
-            vmem(16, 2, 32, 128),
+            vmem(2048, 128),
+            vmem(2, 8, 2, 64, 128),
+            vmem(2, 8, 3, 2, 64, 128),
+            vmem(2, 8, 2, 32, 128),
+            vmem(2, 16, 32, 128),
             vmem(32, 288, 128),
             dma(12),
             dma(15), dma(15),
             dma(12), dma(12),
             dma(16), dma(16),
-            dma(24), dma(24),
-            dma(8), dma(8),
+            dma(48), dma(48),
             dma(16), dma(16),
+            dma(32), dma(32),
             dma(24), dma(24),
             dma(8), dma(8),
             dma(4),
         ],
         compiler_params=pltpu.CompilerParams(
-            collective_id=0, has_side_effects=True, vmem_limit_bytes=40 * MIB
+            collective_id=0, has_side_effects=True, vmem_limit_bytes=VMEM_BYTES
         ),
         name="exchange",
     )(placed, wrows)
 
 
-def match_kernel(prof, poly, main, before, after, sci, out, band, toep):
+def match_kernel(prof, poly, even, odd, before, after, sci, out, band, toep):
     j = pl.program_id(0)
     steps = pl.num_programs(0)
     e, s = lax.axis_index("epoch"), lax.axis_index("strip")
@@ -482,7 +512,7 @@
             toep[k, :, 0:128] = hi
             toep[k, :, 128:256] = lo
 
-    planes = [jnp.where(j > 0, before[0], 0.0)] + [main[p] for p in range(8)]
+    planes = [jnp.where(j > 0, before[0], 0.0)] + [(even, odd)[p % 2][p // 2] for p in range(8)]
     planes.append(jnp.where(j < steps - 1, after[0], 0.0))
     rows = []
     t_hi, t_lo = split_hi_lo(jnp.concatenate(planes, axis=1))
@@ -526,18 +556,19 @@
         in_specs=[
             smem,
             smem,
-            pl.BlockSpec((8, 288, 128), lambda j: (j, 0, 0)),
-            pl.BlockSpec((1, 288, 128), lambda j: (jnp.maximum(8 * j - 1, 0), 0, 0)),
-            pl.BlockSpec((1, 288, 128), lambda j: (jnp.minimum(8 * j + 8, 31), 0, 0)),
+            pl.BlockSpec((4, 288, 128), lambda j: (j, 0, 0)),
+            pl.BlockSpec((4, 288, 128), lambda j: (4 + j, 0, 0)),
+            pl.BlockSpec((1, 288, 128), lambda j: (15 + 4 * j, 0, 0)),
+            pl.BlockSpec((1, 288, 128), lambda j: (4 * j + 4, 0, 0)),
             pl.BlockSpec((8, 256, 128), lambda j: (j, 0, 0)),
         ],
         out_specs=pl.BlockSpec((1, 256, 1024), lambda j: (0, 0, j)),
         scratch_shapes=[pltpu.VMEM((256, 480), BF16), pltpu.VMEM((2, 256, 256), BF16)],
         compiler_params=pltpu.CompilerParams(
-            dimension_semantics=("arbitrary",), vmem_limit_bytes=48 * MIB
+            dimension_semantics=("arbitrary",), vmem_limit_bytes=VMEM_BYTES
         ),
         name="match",
-    )(profiles, poly, template, template, template, science)
+    )(profiles, poly, template, template, template, template, science)
 
 
 def shards(

time: 178 us -> 148 us (0.83)
  the two profiles are of different devices: /device:TPU:1 before, /device:TPU:81 now
where the time goes in v2:
time: 148 us; the launch traced here: 147 us
  Pallas kernels  146 us (99%)
    pallas_call x1, Pallas kernels, exchange(): pl.pallas_call(exchange_kernel, out_shape=(jax.ShapeDtypeStruct((32, 256,...  113 us
    pallas_call x1, Pallas kernels, warp(): pl.pallas_call(warp_kernel, grid=(TILES_DEV,), out_shape=(jax.ShapeDtypeS...  19.2 us
    pallas_call x1, Pallas kernels, match(): pl.pallas_call(match_kernel, grid=(4,), out_shape=jax.ShapeDtypeStruct((1...  13.6 us

profile of v2, /device:TPU:81, one launch (start us, length us, event | category | flops | bytes accessed | tf_op | source)
XLA Modules:
  0.0 147.3 jit_solution(10350003230722826579)
XLA Ops:
  0.0 19.2 %warp.1 = (f32[4,3328,128]{2,1,0:T(8,128)}, f32[32,128]{1,0:T(8,128)}) custom-call(s32[1,12]{1,0:T(1,128)} %kinds.1, s32[1,8,24]{2,1,0:T(8,128)} %heights.1, f32[1,12]{1,0:T(1,128)} %invvar.1, f32[1,12,256,512]{3,2,1,0:T(8,128)} %x_ref.1, f32[4,256,256]{2,1,0:T(8,128)} %r_ref.1, f32[4,512,512]{2,1,0:T(8,128)} %c_ref.1), custom_call_target="tpu_custom_call" | custom-call | tf_op jit(solution)/shard_map/warp/pallas_call | solution.py:90
  19.2 113.1 %exchange.1 = (f32[32,256,128]{2,1,0:T(8,128)}, f32[32,288,128]{2,1,0:T(8,128)}) custom-call(f32[4,3328,128]{2,1,0:T(8,128)} %get-tuple-element.9.placed, f32[32,128]{1,0:T(8,128)} %get-tuple-element.10.wrows), custom_call_target="tpu_custom_call" | custom-call | tf_op jit(solution)/shard_map/exchange/pallas_call | solution.py:445
  132.3 1.4 copy.9.poly
  133.7 13.6 %match.1 = f32[1,256,4096]{2,1,0:T(8,128)} custom-call(f32[2,2,31]{2,1,0:T(2,128)} %prof.1, f32[8,2,6]{2,1,0:T(2,128)} %copy.9.poly, f32[32,288,128]{2,1,0:T(8,128)} %get-tuple-element.11.even.odd.before.after, f32[32,288,128]{2,1,0:T(8,128)} %get-tuple-element.11.even.odd.before.after, f32[32,288,128]{2,1,0:T(8,128)} %get-tuple-element.11.even.odd.before.after, ...), custom_call_target="tpu_custom_call" | custom-call | tf_op jit(solution)/shard_map/match/pallas_call | solution.py:552

commit v3 on v2

--- a/solution.py
+++ b/solution.py
@@ -11,7 +11,7 @@
 BF16 = jnp.bfloat16
 MESH = pl.DeviceIdType.MESH
 TILES_DEV = 12
-PER_COL = 24
+PER_STEP = 2
 LOCAL_ROWS = 3328
 SPAN = 3072
 VMEM_BYTES = 67043328
@@ -40,17 +40,25 @@
 
 
 def warp_kernel(
-    kinds, heights, invvar, x_ref, r_ref, c_ref, placed, wrows, r_hi, r_lo, c_hi, c_lo, tops
+    kinds, heights, invvar, x_ref, r_hbm, c_hbm, out, wrows,
+    r_f32, c_f32, r_cat, c_cat, placed, tops, r_sem, c_sem, out_sem,
 ):
     t = pl.program_id(0)
     strip = lax.axis_index("strip")
     block, side = strip // 2, strip % 2
 
+    def piece(i):
+        rows = pl.ds(i * 256, 256)
+        return pltpu.make_async_copy(placed.at[:, rows, :], out.at[:, rows, :], out_sem.at[i])
+
     @pl.when(t == 0)
     def _():
+        loads = []
         for k in range(4):
-            r_hi[k], r_lo[k] = split_hi_lo(r_ref[k])
-            c_hi[k], c_lo[k] = split_hi_lo(c_ref[k])
+            loads.append(pltpu.make_async_copy(c_hbm.at[k], c_f32.at[k], c_sem.at[k]))
+            loads.append(pltpu.make_async_copy(r_hbm.at[k], r_f32.at[k], r_sem.at[k]))
+        for load in loads:
+            load.start()
         placed[...] = jnp.zeros_like(placed)
 
         def above(i, top):
@@ -60,55 +68,87 @@
 
             return top + heights[0, block, i]
 
-        lax.fori_loop(0, (side + 1) * TILES_DEV, above, jnp.int32(0))
+        tops[TILES_DEV] = lax.fori_loop(0, (side + 1) * TILES_DEV, above, jnp.int32(0))
         row = lax.broadcasted_iota(jnp.int32, (32, 128), 0) * 128
         row = row + lax.broadcasted_iota(jnp.int32, (32, 128), 1)
 
         def weigh(i, acc):
-            top = tops[i]
-            live = (row >= top) & (row < top + heights[0, block, side * TILES_DEV + i])
+            live = (row >= tops[i]) & (row < tops[i + 1])
             return jnp.where(live, invvar[0, i], acc)
 
         wrows[...] = lax.fori_loop(0, TILES_DEV, weigh, jnp.zeros((32, 128), F32))
-
-    kind = kinds[0, t]
-    height = heights[0, block, side * TILES_DEV + t]
-    top = tops[t] - side * 1024
-    live = lax.broadcasted_iota(jnp.int32, (256, 512), 0) < height
-    x_hi, x_lo = split_hi_lo(jnp.where(live, x_ref[0, 0], 0.0))
-    y = dot_t(x_hi, c_hi[kind]) + (dot_t(x_hi, c_lo[kind]) + dot_t(x_lo, c_hi[kind]))
-    y_hi, y_lo = split_hi_lo(y)
-    w = dot(r_hi[kind], y_hi) + (dot(r_hi[kind], y_lo) + dot(r_lo[kind], y_hi))
-    w = jnp.where(live, w, 0.0)
-    for p in range(4):
-        placed[p, pl.ds(top, 256), :] = w[:, p * 128 : (p + 1) * 128]
+        for k in range(4):
+            loads[2 * k].wait()
+            hi, lo = split_hi_lo(c_f32[k].T)
+            for i, part in enumerate((hi, lo, hi)):
+                c_cat[k, 512 * i : 512 * i + 512, :] = part
+            loads[2 * k + 1].wait()
+            hi, lo = split_hi_lo(r_f32[k])
+            for i, part in enumerate((hi, hi, lo)):
+                r_cat[k, :, 256 * i : 256 * i + 256] = part
+
+    places = []
+    for i in range(PER_STEP):
+        n = PER_STEP * t + i
+        kind, top = kinds[0, n], tops[n] - side * 1024
+        live = lax.broadcasted_iota(jnp.int32, (256, 512), 0) < tops[n + 1] - tops[n]
+        hi, lo = split_hi_lo(jnp.where(live, x_ref[0, i], 0.0))
+        y = dot(jnp.concatenate([hi, hi, lo], axis=1), c_cat[kind])
+        places.append((kind, top, live, y))
+    warped = []
+    for kind, top, live, y in places:
+        hi, lo = split_hi_lo(y)
+        w = dot(r_cat[kind], jnp.concatenate([hi, lo, hi], axis=0))
+        warped.append(jnp.where(live, w, 0.0))
+    for (kind, top, live, y), w in zip(places, warped):
+        for p in range(4):
+            placed[p, pl.ds(top, 256), :] = w[:, p * 128 : (p + 1) * 128]
+
+    last = t == pl.num_programs(0) - 1
+    start, end = tops[PER_STEP * t], tops[PER_STEP * (t + 1)]
+    first = jnp.where(t == 0, 0, (start - side * 1024) // 256)
+    ready = jnp.where(last, 12, jnp.minimum((end - side * 1024) // 256, 12))
+
+    @pl.loop(first, ready)
+    def _(i):
+        piece(i).start()
+
+    @pl.when(last)
+    def _():
+        @pl.loop(0, 12)
+        def _(i):
+            piece(i).wait()
 
 
 def warp(raw_tiles, tile_kind, tile_invvar, tile_heights, row_interp, col_interp):
     smem = pl.BlockSpec(memory_space=pltpu.SMEM)
-    whole = lambda shape: pl.BlockSpec(shape, lambda t: (0,) * len(shape))
+    anywhere = pl.BlockSpec(memory_space=pl.ANY)
     return pl.pallas_call(
         warp_kernel,
-        grid=(TILES_DEV,),
+        grid=(TILES_DEV // PER_STEP,),
         out_shape=(
-            jax.ShapeDtypeStruct((4, LOCAL_ROWS, 128), F32),
+            jax.ShapeDtypeStruct((4, SPAN, 128), F32),
             jax.ShapeDtypeStruct((32, 128), F32),
         ),
         in_specs=[
             smem,
             smem,
             smem,
-            pl.BlockSpec((1, 1, 256, 512), lambda t: (0, t, 0, 0)),
-            whole((4, 256, 256)),
-            whole((4, 512, 512)),
+            pl.BlockSpec((1, PER_STEP, 256, 512), lambda t: (0, t, 0, 0)),
+            anywhere,
+            anywhere,
         ],
-        out_specs=(whole((4, LOCAL_ROWS, 128)), whole((32, 128))),
+        out_specs=(anywhere, pl.BlockSpec((32, 128), lambda t: (0, 0))),
         scratch_shapes=[
-            pltpu.VMEM((4, 256, 256), BF16),
-            pltpu.VMEM((4, 256, 256), BF16),
-            pltpu.VMEM((4, 512, 512), BF16),
-            pltpu.VMEM((4, 512, 512), BF16),
-            pltpu.SMEM((TILES_DEV,), jnp.int32),
+            pltpu.VMEM((4, 256, 256), F32),
+            pltpu.VMEM((4, 512, 512), F32),
+            pltpu.VMEM((4, 256, 768), BF16),
+            pltpu.VMEM((4, 1536, 512), BF16),
+            pltpu.VMEM((4, LOCAL_ROWS, 128), F32),
+            pltpu.SMEM((TILES_DEV + 1,), jnp.int32),
+            pltpu.SemaphoreType.DMA((4,)),
+            pltpu.SemaphoreType.DMA((4,)),
+            pltpu.SemaphoreType.DMA((12,)),
         ],
         compiler_params=pltpu.CompilerParams(
             dimension_semantics=("arbitrary",), vmem_limit_bytes=VMEM_BYTES
@@ -118,7 +158,7 @@
 
 
 def exchange_kernel(
-    placed, wrows, sci, t_out, kept, prec, pb, wn, wbuf, wi, sbuf, rbuf, zr, tt, tb,
+    placed, wrows, prof, sci, t_out, band, toep, kept, prec, pb, wn, wbuf, wi, sbuf, rbuf, zr, tt, tb,
     kept_sem, w_s, w_r, pair_s, pair_r, sci_s, sci_r, rs_s, rs_r, z_s, z_r,
     rel_s, rel_r, ag_s, ag_r, halo_s, halo_r, out_sem,
 ):
@@ -351,6 +391,27 @@
 
             pltpu.make_async_copy(tb.at[planes], t_out.at[planes], out_sem.at[j]).start()
 
+    def taps(offset, k, axis):
+        acc = jnp.zeros(offset.shape, F32)
+        for i in range(31):
+            acc = jnp.where(offset == i, prof[k, axis, i], acc)
+        return acc
+
+    def build_bands():
+        iota = lambda shape, axis: lax.broadcasted_iota(jnp.int32, shape, axis)
+        lane = iota((128, 480), 1)
+        section = jnp.where(lane >= 320, 2, jnp.where(lane >= 160, 1, 0))
+        offset = lane - 160 * section - iota((128, 480), 0) - 1
+        m = iota((256, 128), 0)
+        offset_c = jnp.where(m < 192, m, m - 256) - iota((256, 128), 1) + 15
+        for k in range(2):
+            hi, lo = split_hi_lo(taps(offset, k, 0))
+            both = jnp.where(section == 1, lo.astype(F32), hi.astype(F32))
+            band[128 * k : 128 * k + 128, :] = both.astype(BF16)
+            hi, lo = split_hi_lo(taps(offset_c, k, 1))
+            toep[k, :, 0:128] = hi
+            toep[k, :, 128:256] = lo
+
     send_rows(0)
     pltpu.make_async_copy(slab(pb, s), sci.at[pl.ds(2 * s, 2)], sci_r.at[s]).start()
     ring_step(0, 0)
@@ -375,6 +436,7 @@
         row = jnp.broadcast_to(wbuf[15, pl.ds(2 * r + q // 4, 1), :], (128, 128))
         wi[pl.ds(128 * r, 128), :] = row.T
 
+    build_bands()
     ring_step(0, 2)
     send_rows(3)
     ring_step(1, 0)
@@ -439,7 +501,7 @@
             wait_on(tb.at[0:8, 0:16, :], halo_s.at[4 + j])
 
 
-def exchange(placed, wrows):
+def exchange(placed, wrows, profiles):
     vmem = lambda *shape: pltpu.VMEM(shape, F32)
     dma = lambda count: pltpu.SemaphoreType.DMA((count,))
     return pl.pallas_call(
@@ -447,12 +509,20 @@
         out_shape=(
             jax.ShapeDtypeStruct((32, 256, 128), F32),
             jax.ShapeDtypeStruct((32, 288, 128), F32),
+            jax.ShapeDtypeStruct((256, 480), BF16),
+            jax.ShapeDtypeStruct((2, 256, 256), BF16),
         ),
         in_specs=[
             pl.BlockSpec(memory_space=pl.ANY),
             pl.BlockSpec(memory_space=pltpu.VMEM),
+            pl.BlockSpec(memory_space=pltpu.SMEM),
         ],
-        out_specs=(pl.BlockSpec(memory_space=pl.ANY), pl.BlockSpec(memory_space=pl.ANY)),
+        out_specs=(
+            pl.BlockSpec(memory_space=pl.ANY),
+            pl.BlockSpec(memory_space=pl.ANY),
+            pl.BlockSpec(memory_space=pltpu.VMEM),
+            pl.BlockSpec(memory_space=pltpu.VMEM),
+        ),
         scratch_shapes=[
             vmem(2, SPAN, 128),
             vmem(2, SPAN, 128),
@@ -480,37 +550,13 @@
             collective_id=0, has_side_effects=True, vmem_limit_bytes=VMEM_BYTES
         ),
         name="exchange",
-    )(placed, wrows)
-
-
-def match_kernel(prof, poly, even, odd, before, after, sci, out, band, toep):
+    )(placed, wrows, profiles)
+
+
+def match_kernel(band, toep, poly, even, odd, before, after, sci, out):
     j = pl.program_id(0)
     steps = pl.num_programs(0)
     e, s = lax.axis_index("epoch"), lax.axis_index("strip")
-
-    def taps(offset, k, axis):
-        def add(i, acc):
-            return jnp.where(offset == i, prof[k, axis, i], acc)
-
-        return lax.fori_loop(0, 31, add, jnp.zeros(offset.shape, F32), unroll=True)
-
-    @pl.when(j == 0)
-    def _():
-        lane = lax.broadcasted_iota(jnp.int32, (128, 480), 1)
-        section = (lane >= 160).astype(jnp.int32) + (lane >= 320).astype(jnp.int32)
-        offset = lane - 160 * section - lax.broadcasted_iota(jnp.int32, (128, 480), 0) - 1
-        for k in range(2):
-            hi, lo = split_hi_lo(taps(offset, k, 0))
-            band[128 * k : 128 * k + 128, :] = jnp.where(
-                section == 1, lo.astype(F32), hi.astype(F32)
-            ).astype(BF16)
-        m = lax.broadcasted_iota(jnp.int32, (256, 128), 0)
-        source = jnp.where(m < 192, m, m - 256)
-        offset = source - lax.broadcasted_iota(jnp.int32, (256, 128), 1) + 15
-        for k in range(2):
-            hi, lo = split_hi_lo(taps(offset, k, 1))
-            toep[k, :, 0:128] = hi
-            toep[k, :, 128:256] = lo
 
     planes = [jnp.where(j > 0, before[0], 0.0)] + [(even, odd)[p % 2][p // 2] for p in range(8)]
     planes.append(jnp.where(j < steps - 1, after[0], 0.0))
@@ -547,14 +593,15 @@
         )
 
 
-def match(profiles, poly, template, science):
+def match(band, toep, poly, template, science):
     smem = pl.BlockSpec(memory_space=pltpu.SMEM)
     return pl.pallas_call(
         match_kernel,
         grid=(4,),
         out_shape=jax.ShapeDtypeStruct((1, 256, 4096), F32),
         in_specs=[
-            smem,
+            pl.BlockSpec((256, 480), lambda j: (0, 0)),
+            pl.BlockSpec((2, 256, 256), lambda j: (0, 0, 0)),
             smem,
             pl.BlockSpec((4, 288, 128), lambda j: (j, 0, 0)),
             pl.BlockSpec((4, 288, 128), lambda j: (4 + j, 0, 0)),
@@ -563,12 +610,11 @@
             pl.BlockSpec((8, 256, 128), lambda j: (j, 0, 0)),
         ],
         out_specs=pl.BlockSpec((1, 256, 1024), lambda j: (0, 0, j)),
-        scratch_shapes=[pltpu.VMEM((256, 480), BF16), pltpu.VMEM((2, 256, 256), BF16)],
         compiler_params=pltpu.CompilerParams(
             dimension_semantics=("arbitrary",), vmem_limit_bytes=VMEM_BYTES
         ),
         name="match",
-    )(profiles, poly, template, template, template, template, science)
+    )(band, toep, poly, template, template, template, template, science)
 
 
 def shards(
@@ -577,8 +623,8 @@
     placed, wrows = warp(
         raw_tiles, tile_kind, tile_invvar, tile_heights, row_interp, col_interp
     )
-    science, template = exchange(placed, wrows)
-    return match(psf_profiles, psf_poly, template, science)
+    science, template, band, toep = exchange(placed, wrows, psf_profiles)
+    return match(band, toep, psf_poly, template, science)
 
 
 def solution(mesh):

time: 148 us -> 142 us (0.959)
  Pallas kernels: 146 us -> 140 us
    pallas_call x1, Pallas kernels: 19.2 us -> 15.3 us  [warp(): pl.pallas_call(warp_kernel, grid=(TILES_DEV // PER_STEP,), out_shape=(jax...]
    pallas_call x1, Pallas kernels: 13.6 us -> 11.5 us  [match(): pl.pallas_call(match_kernel, grid=(4,), out_shape=jax.ShapeDtypeStruct((1...]
where the time goes in v3:
time: 142 us
  Pallas kernels  140 us (99%)
    pallas_call x1, Pallas kernels, exchange(): pl.pallas_call(exchange_kernel, out_shape=(jax.ShapeDtypeStruct((32, 256,...  113 us
    pallas_call x1, Pallas kernels, warp(): pl.pallas_call(warp_kernel, grid=(TILES_DEV // PER_STEP,), out_shape=(jax...  15.3 us
    pallas_call x1, Pallas kernels, match(): pl.pallas_call(match_kernel, grid=(4,), out_shape=jax.ShapeDtypeStruct((1...  11.5 us

profile of v3, /device:TPU:81, one launch (start us, length us, event | category | flops | bytes accessed | tf_op | source)
XLA Modules:
  0.0 141.6 jit_solution(12206729352834883318)
XLA Ops:
  0.0 15.3 %warp.1 = (f32[4,3072,128]{2,1,0:T(8,128)}, f32[32,128]{1,0:T(8,128)}) custom-call(s32[1,12]{1,0:T(1,128)} %kinds.1, s32[1,8,24]{2,1,0:T(8,128)} %heights.1, f32[1,12]{1,0:T(1,128)} %invvar.1, f32[1,12,256,512]{3,2,1,0:T(8,128)} %x_ref.1, f32[4,256,256]{2,1,0:T(8,128)} %r_hbm.1, f32[4,512,512]{2,1,0:T(8,128)} %c_hbm.1), custom_call_target="tpu_custom_call" | custom-call | tf_op jit(solution)/shard_map/warp/pallas_call | solution.py:126
  15.3 113.3 %exchange.1 = (f32[32,256,128]{2,1,0:T(8,128)}, f32[32,288,128]{2,1,0:T(8,128)}, bf16[256,480]{1,0:T(8,128)(2,1)}, bf16[2,256,256]{2,1,0:T(8,128)(2,1)}) custom-call(f32[4,3072,128]{2,1,0:T(8,128)} %get-tuple-element.11.placed, f32[32,128]{1,0:T(8,128)} %get-tuple-element.12.wrows, f32[2,2,31]{2,1,0:T(2,128)} %prof.1), custom_call_target="tpu_custom_call" | custom-call | tf_op jit(solution)/shard_map/exchange/pallas_call | solution.py:507
  128.6 1.4 copy.9.poly
  130.0 11.5 %match.1 = f32[1,256,4096]{2,1,0:T(8,128)} custom-call(bf16[256,480]{1,0:T(8,128)(2,1)} %get-tuple-element.13.band, bf16[2,256,256]{2,1,0:T(8,128)(2,1)} %get-tuple-element.14.toep, f32[8,2,6]{2,1,0:T(2,128)} %copy.9.poly, f32[32,288,128]{2,1,0:T(8,128)} %get-tuple-element.15.even.odd.before.after, f32[32,288,128]{2,1,0:T(8,128)} %get-tuple-element.15.even.odd.before.after, ...), custom_call_target="tpu_custom_call" | custom-call | tf_op jit(solution)/shard_map/match/pallas_call | solution.py:598

commit v4 on v3

--- a/solution.py
+++ b/solution.py
@@ -203,10 +203,12 @@
         ).start()
     pl.semaphore_wait(barrier, 29)
 
-    for k in range(1, 16):
+    def send_weights(k):
         epoch = (e + k % 8) % 8
         strip = s if k < 8 else pair
         send(wrows, wbuf.at[15 - k], w_s.at[k - 1], w_r.at[15 - k], epoch, strip)
+
+    send_weights(8)
 
     def piece_at(k):
         return (s // 2 + k // 2) % 8 * 2 + k % 2
@@ -221,6 +223,9 @@
                 placed.at[pl.ds(2 * (1 - c), 2), pl.ds(i * 256, 256), :],
                 slab(prec, i), pair_s.at[i], pair_r.at[i], e, pair,
             )
+
+    for k in (1, 2, 3, 4, 5, 6, 7, 9, 10, 11, 12, 13, 14, 15):
+        send_weights(k)
 
     wait_on(wbuf.at[7], w_r.at[7])
     wbuf[15] = wrows[...] + wbuf[7]
@@ -347,19 +352,20 @@
 
     def gather_far(h):
         for j in (2 * h, 2 * h + 1):
-            wait_on(seg(j, 64 * left + 32 * zl, 32), ag_r.at[4 + j])
-            wait_on(seg(j, 64 * left + 32 * (1 - zl), 32), ag_r.at[12 + j])
-            wait_on(seg(j, 64 * right + 32 * zl, 32), ag_r.at[8 + j])
-            wait_on(seg(j, 64 * right + 32 * (1 - zl), 32), ag_r.at[16 + j])
             if j % 2 == 0:
-                part = seg(j, 64 * left, 64)
-                send(part, part, ag_s.at[20 + j], ag_r.at[20 + j], x_right, s)
+                side, to, at = left, x_right, 4
             else:
-                part = seg(j, 64 * right, 64)
-                send(part, part, ag_s.at[20 + j], ag_r.at[20 + j], x_left, s)
+                side, to, at = right, x_left, 8
+            wait_on(seg(j, 64 * side + 32 * zl, 32), ag_r.at[at + j])
+            wait_on(seg(j, 64 * side + 32 * (1 - zl), 32), ag_r.at[at + 8 + j])
+            part = seg(j, 64 * side, 64)
+            send(part, part, ag_s.at[20 + j], ag_r.at[20 + j], to, s)
 
     def edges(h):
         for j in (2 * h, 2 * h + 1):
+            side, at = (right, 8) if j % 2 == 0 else (left, 4)
+            wait_on(seg(j, 64 * side + 32 * zl, 32), ag_r.at[at + j])
+            wait_on(seg(j, 64 * side + 32 * (1 - zl), 32), ag_r.at[at + 8 + j])
             wait_on(seg(j, 64 * ((x + 2) % 4), 64), ag_r.at[20 + j])
             planes = pl.ds(8 * j, 8)
 
@@ -580,7 +586,7 @@
         conv.append(first[:, :128] + (first[:, 128:] + dot(lo, toep[k, :, 0:128])))
     row = lax.broadcasted_iota(jnp.int32, (256, 128), 0) + s * 256
     u = (2.0 * row.astype(F32) + 1.0) / 4096.0 - 1.0
-    terms = [[poly[e, k, i] for i in range(6)] for k in range(2)]
+    terms = [[poly[i, k, e] for i in range(6)] for k in range(2)]
     base = [t[0] + t[1] * u + t[3] * u * u for t in terms]
     slope = [t[2] + t[4] * u for t in terms]
     for p in range(8):
@@ -624,7 +630,7 @@
         raw_tiles, tile_kind, tile_invvar, tile_heights, row_interp, col_interp
     )
     science, template, band, toep = exchange(placed, wrows, psf_profiles)
-    return match(band, toep, psf_poly, template, science)
+    return match(band, toep, jnp.transpose(psf_poly, (2, 1, 0)), template, science)
 
 
 def solution(mesh):

time: 142 us -> 141 us (level)
  no operation moved by 1% of the time
where the time goes in v4:
time: 141 us; the launch traced here: 140 us
  Pallas kernels  140 us (99%)
    pallas_call x1, Pallas kernels, exchange(): pl.pallas_call(exchange_kernel, out_shape=(jax.ShapeDtypeStruct((32, 256,...  113 us
    pallas_call x1, Pallas kernels, warp(): pl.pallas_call(warp_kernel, grid=(TILES_DEV // PER_STEP,), out_shape=(jax...  15.3 us
    pallas_call x1, Pallas kernels, match(): pl.pallas_call(match_kernel, grid=(4,), out_shape=jax.ShapeDtypeStruct((1...  11.6 us

profile of v4, /device:TPU:81, one launch (start us, length us, event | category | flops | bytes accessed | tf_op | source)
XLA Modules:
  0.0 140.2 jit_solution(5879298776398628090)
XLA Ops:
  0.0 15.3 %warp.1 = (f32[4,3072,128]{2,1,0:T(8,128)}, f32[32,128]{1,0:T(8,128)}) custom-call(s32[1,12]{1,0:T(1,128)} %kinds.1, s32[1,8,24]{2,1,0:T(8,128)} %heights.1, f32[1,12]{1,0:T(1,128)} %invvar.1, f32[1,12,256,512]{3,2,1,0:T(8,128)} %x_ref.1, f32[4,256,256]{2,1,0:T(8,128)} %r_hbm.1, f32[4,512,512]{2,1,0:T(8,128)} %c_hbm.1), custom_call_target="tpu_custom_call" | custom-call | tf_op jit(solution)/shard_map/warp/pallas_call | solution.py:126
  15.3 113.3 %exchange.1 = (f32[32,256,128]{2,1,0:T(8,128)}, f32[32,288,128]{2,1,0:T(8,128)}, bf16[256,480]{1,0:T(8,128)(2,1)}, bf16[2,256,256]{2,1,0:T(8,128)(2,1)}) custom-call(f32[4,3072,128]{2,1,0:T(8,128)} %get-tuple-element.11.placed, f32[32,128]{1,0:T(8,128)} %get-tuple-element.12.wrows, f32[2,2,31]{2,1,0:T(2,128)} %prof.1), custom_call_target="tpu_custom_call" | custom-call | tf_op jit(solution)/shard_map/exchange/pallas_call | solution.py:513
  128.6 11.6 %match.1 = f32[1,256,4096]{2,1,0:T(8,128)} custom-call(bf16[256,480]{1,0:T(8,128)(2,1)} %get-tuple-element.13.band, bf16[2,256,256]{2,1,0:T(8,128)(2,1)} %get-tuple-element.14.toep, f32[6,2,8]{2,1,0:T(2,128)} %bitcast.1, f32[32,288,128]{2,1,0:T(8,128)} %get-tuple-element.15.even.odd.before.after, f32[32,288,128]{2,1,0:T(8,128)} %get-tuple-element.15.even.odd.before.after, ...), custom_call_target="tpu_custom_call" | custom-call | tf_op jit(solution)/shard_map/match/pallas_call | solution.py:604

commit v5 on v4

--- a/solution.py
+++ b/solution.py
@@ -11,7 +11,7 @@
 BF16 = jnp.bfloat16
 MESH = pl.DeviceIdType.MESH
 TILES_DEV = 12
-PER_STEP = 2
+PER_STEP = 3
 LOCAL_ROWS = 3328
 SPAN = 3072
 VMEM_BYTES = 67043328

time: 141 us -> 140 us (level)
  no operation moved by 1% of the time
where the time goes in v5:
time: 140 us
  Pallas kernels  140 us (100%)
    pallas_call x1, Pallas kernels, exchange(): pl.pallas_call(exchange_kernel, out_shape=(jax.ShapeDtypeStruct((32, 256,...  114 us
    pallas_call x1, Pallas kernels, warp(): pl.pallas_call(warp_kernel, grid=(TILES_DEV // PER_STEP,), out_shape=(jax...  15 us
    pallas_call x1, Pallas kernels, match(): pl.pallas_call(match_kernel, grid=(4,), out_shape=jax.ShapeDtypeStruct((1...  11.6 us

profile of v5, /device:TPU:81, one launch (start us, length us, event | category | flops | bytes accessed | tf_op | source)
XLA Modules:
  0.0 140.1 jit_solution(547136037196947579)
XLA Ops:
  0.0 15.0 %warp.1 = (f32[4,3072,128]{2,1,0:T(8,128)}, f32[32,128]{1,0:T(8,128)}) custom-call(s32[1,12]{1,0:T(1,128)} %kinds.1, s32[1,8,24]{2,1,0:T(8,128)} %heights.1, f32[1,12]{1,0:T(1,128)} %invvar.1, f32[1,12,256,512]{3,2,1,0:T(8,128)} %x_ref.1, f32[4,256,256]{2,1,0:T(8,128)} %r_hbm.1, f32[4,512,512]{2,1,0:T(8,128)} %c_hbm.1), custom_call_target="tpu_custom_call" | custom-call | tf_op jit(solution)/shard_map/warp/pallas_call | solution.py:126
  15.0 113.6 %exchange.1 = (f32[32,256,128]{2,1,0:T(8,128)}, f32[32,288,128]{2,1,0:T(8,128)}, bf16[256,480]{1,0:T(8,128)(2,1)}, bf16[2,256,256]{2,1,0:T(8,128)(2,1)}) custom-call(f32[4,3072,128]{2,1,0:T(8,128)} %get-tuple-element.11.placed, f32[32,128]{1,0:T(8,128)} %get-tuple-element.12.wrows, f32[2,2,31]{2,1,0:T(2,128)} %prof.1), custom_call_target="tpu_custom_call" | custom-call | tf_op jit(solution)/shard_map/exchange/pallas_call | solution.py:513
  128.5 11.6 %match.1 = f32[1,256,4096]{2,1,0:T(8,128)} custom-call(bf16[256,480]{1,0:T(8,128)(2,1)} %get-tuple-element.13.band, bf16[2,256,256]{2,1,0:T(8,128)(2,1)} %get-tuple-element.14.toep, f32[6,2,8]{2,1,0:T(2,128)} %bitcast.1, f32[32,288,128]{2,1,0:T(8,128)} %get-tuple-element.15.even.odd.before.after, f32[32,288,128]{2,1,0:T(8,128)} %get-tuple-element.15.even.odd.before.after, ...), custom_call_target="tpu_custom_call" | custom-call | tf_op jit(solution)/shard_map/match/pallas_call | solution.py:604
